TPU v7x, 32 devices: a whole 2x2x4 slice. The times are simulated.
32 devices in a mesh: seq: 8 (over y, x, core), doc: 4 (over z).
Axes of the slice: x: 2, y: 2, z: 4, core: 2. Of those that a mesh axis runs over, the one named last changes fastest.
Arguments:
- tokens: bfloat16 [4, 4096, 1024], P('doc', 'seq'), may hold values from -6 to 6
- cotangent: bfloat16 [4, 4096, 1024], P('doc', 'seq'), may hold values from -6 to 6
- attn_gain: bfloat16 [1024], replicated, may hold values from 0.5 to 1.5
- w_query: bfloat16 [1024, 1024], replicated, may hold values from -0.1875 to 0.1875
- w_key: bfloat16 [1024, 1024], replicated, may hold values from -0.1875 to 0.1875
- w_value: bfloat16 [1024, 1024], replicated, may hold values from -0.1875 to 0.1875
- w_out: bfloat16 [1024, 1024], replicated, may hold values from -3 to 3
- ffn_gain: bfloat16 [1024], replicated, may hold values from 0.5 to 1.5
- w_gate: bfloat16 [1024, 2816], replicated, may hold values from -0.1875 to 0.1875
- w_up: bfloat16 [1024, 2816], replicated, may hold values from -0.1875 to 0.1875
- w_down: bfloat16 [2816, 1024], replicated, may hold values from -0.109375 to 0.109375
- mem_keys: bfloat16 [4, 4096, 1024], P('doc', 'seq'), may hold values from -6 to 6
- mem_values: bfloat16 [4, 4096, 1024], P('doc', 'seq'), may hold values from -6 to 6
- seg_len: int32 [4, 2], P('doc'), may hold values from 512 to 2048, as said below
- mem_idx: int32 [4, 8, 128], P('doc', 'seq'), may hold values from 0 to 4095, as said below
Outputs:
- layer_out: bfloat16 [4, 4096, 1024], P('doc', 'seq')
- grad_tokens: bfloat16 [4, 4096, 1024], P('doc', 'seq')
- grad_attn_gain: float32 [1024], P(('seq', 'doc'))
- grad_query: float32 [1024, 1024], P(('seq', 'doc'))
- grad_key: float32 [1024, 1024], P(('seq', 'doc'))
- grad_value: float32 [1024, 1024], P(('seq', 'doc'))
- grad_out: float32 [1024, 1024], P(('seq', 'doc'))
- grad_ffn_gain: float32 [1024], P(('seq', 'doc'))
- grad_gate: float32 [1024, 2816], P(('seq', 'doc'))
- grad_up: float32 [1024, 2816], P(('seq', 'doc'))
- grad_down: float32 [2816, 1024], P(('seq', 'doc'))
- grad_mem_keys: float32 [4, 4096, 1024], P('doc', 'seq')
- grad_mem_values: float32 [4, 4096, 1024], P('doc', 'seq')
Inputs may be any that keep to these rules, and one draw needn't show every extreme that they name: Positions at or beyond seg_len in a segment are padding; in every stream some segment has all 2048 positions valid. `mem_idx`: memory row r of a stream lies on seq index r // 512. Each query block names exactly 32 distinct rows of each of half of the seq indices and none of the others; which indices is drawn afresh for every block.
All inputs are finite; a program needn't handle non-finite values.
Results may differ from a plain program's by a relative error of at most 0.014.
Values may be sent and summed in bfloat16 or wider, within the bound.
A program may use at most 320 MiB of HBM per device.

v0:
```python
import jax
import jax.numpy as jnp
from jax import lax
from jax.sharding import PartitionSpec as P

HEADS = 8
HEAD_DIM = 128
TOPK = 128
BPS = 4


EPS = 1e-05
NEG = -1000000000.0


def from_behind(value, axis, steps):
    count = lax.axis_size(axis)
    leading, last = (max(0, -steps), min(count, count - steps))
    return lax.ppermute(value, axis, [(source, source + steps) for source in range(leading, last)])


def rms_factor(values):
    return lax.rsqrt(jnp.mean(values * values, axis=-1, keepdims=True) + EPS)


def neighbour_blocks(kv_own):
    pieces = []
    for distance in range(BPS - 1, 0, -1):
        pieces.append(from_behind(kv_own, "seq", distance))
    pieces.append(kv_own)
    return jnp.concatenate(pieces, axis=2)


def take_rows(table, row_ids):
    return jnp.take(table, row_ids, axis=0)


def add_rows(table, row_ids, updates):
    return table.at[row_ids].add(updates)


def fetch_rows(mem_keys, mem_values, row_ids, owner_count, capacity):
    stream_count = mem_keys.shape[0]
    key_rows = jax.vmap(take_rows)(mem_keys, row_ids)
    value_rows = jax.vmap(take_rows)(mem_values, row_ids)
    stacked = jnp.stack((key_rows, value_rows), axis=1)
    stacked = stacked.reshape(stack_shape(stream_count, owner_count, capacity, mem_keys.shape[2]))
    arrived = lax.all_to_all(stacked, "seq", split_axis=2, concat_axis=2, tiled=True)
    return arrived.reshape(stream_count, 2, owner_count * capacity, mem_keys.shape[2])


def stack_shape(stream_count, owner_count, capacity, attn_width):
    return (stream_count, 2, owner_count, capacity, attn_width)


def attention_scores(queries, kv_seg, mem_kv, allowed):
    count = queries.shape[0]
    key_rows = jnp.concatenate((kv_seg[0], mem_kv[0]), axis=0)
    value_rows = jnp.concatenate((kv_seg[1], mem_kv[1]), axis=0)
    qheads = queries.reshape(count, HEADS, HEAD_DIM)
    kheads = key_rows.reshape(key_rows.shape[0], HEADS, HEAD_DIM)
    vheads = value_rows.reshape(value_rows.shape[0], HEADS, HEAD_DIM)
    logits = jnp.einsum(
        "qhd,khd->hqk", qheads, kheads, preferred_element_type=jnp.float32
    ) * HEAD_DIM ** (-0.5)
    return (jnp.where(allowed[None], logits, NEG), qheads, kheads, vheads)


def attend_forward(operands):
    queries, kv_seg, mem_kv, allowed = operands
    scores, qheads, kheads, vheads = attention_scores(queries, kv_seg, mem_kv, allowed)
    row_max = jnp.max(scores, axis=-1, keepdims=True)
    exponent = jnp.exp(scores - row_max)
    total = jnp.sum(exponent, axis=-1, keepdims=True)
    weights = (exponent / total).astype(jnp.bfloat16)
    attended = jnp.einsum("hqk,khd->qhd", weights, vheads, preferred_element_type=jnp.float32)
    return (attended.reshape(queries.shape[0], -1), (row_max + jnp.log(total))[..., 0])


def attend_backward(operands):
    queries, kv_seg, mem_kv, allowed, log_total, grad_rows = operands
    scores, qheads, kheads, vheads = attention_scores(queries, kv_seg, mem_kv, allowed)
    weights = jnp.exp(scores - log_total[..., None])
    grad_heads = grad_rows.reshape(grad_rows.shape[0], HEADS, HEAD_DIM)
    grad_weights = jnp.einsum(
        "qhd,khd->hqk", grad_heads, vheads, preferred_element_type=jnp.float32
    )
    inner = jnp.sum(weights * grad_weights, axis=-1, keepdims=True)
    grad_scores = (weights * (grad_weights - inner)).astype(jnp.bfloat16)
    scale = HEAD_DIM ** (-0.5)
    grad_queries = (
        jnp.einsum("hqk,khd->qhd", grad_scores, kheads, preferred_element_type=jnp.float32) * scale
    )
    grad_keys = (
        jnp.einsum("hqk,qhd->khd", grad_scores, qheads, preferred_element_type=jnp.float32) * scale
    )
    grad_values = jnp.einsum(
        "hqk,qhd->khd", weights.astype(jnp.bfloat16), grad_heads, preferred_element_type=jnp.float32
    )
    attn_width = queries.shape[1]
    return (
        grad_queries.reshape(queries.shape[0], attn_width),
        grad_keys.reshape(-1, attn_width),
        grad_values.reshape(-1, attn_width),
    )


def on_device(
    tokens,
    cotangent,
    attn_gain,
    w_query,
    w_key,
    w_value,
    w_out,
    ffn_gain,
    w_gate,
    w_up,
    w_down,
    mem_keys,
    mem_values,
    seg_len,
    mem_idx,
):
    stream_count, block_len, model_width = tokens.shape
    attn_width = w_query.shape[1]
    mem_rows = mem_keys.shape[1]
    seq_count = lax.axis_size("seq")
    place = lax.axis_index("seq")
    part_pos = place % BPS
    segment = place // BPS
    capacity = 2 * TOPK // seq_count
    slot_count = seq_count * capacity
    seg_width = BPS * block_len
    lengths = lax.dynamic_index_in_dim(seg_len, segment, 1, keepdims=False)
    tokens_f = tokens.astype(jnp.float32).reshape(-1, model_width)
    gain_one = attn_gain.astype(jnp.float32)
    gain_two = ffn_gain.astype(jnp.float32)
    factor_one = rms_factor(tokens_f)
    unit_one = tokens_f * factor_one
    normed_one = (unit_one * gain_one).astype(jnp.bfloat16)
    queries = jnp.dot(normed_one, w_query, preferred_element_type=jnp.float32).astype(jnp.bfloat16)
    keys_own = jnp.dot(normed_one, w_key, preferred_element_type=jnp.float32).astype(jnp.bfloat16)
    values_own = jnp.dot(normed_one, w_value, preferred_element_type=jnp.float32).astype(
        jnp.bfloat16
    )
    kv_own = jnp.stack(
        (
            keys_own.reshape(stream_count, block_len, attn_width),
            values_own.reshape(stream_count, block_len, attn_width),
        ),
        axis=1,
    )
    kv_seg = neighbour_blocks(kv_own)
    chosen = mem_idx[:, 0, :]
    owner = chosen // mem_rows
    local_row = chosen % mem_rows
    order = jnp.arange(TOPK)
    same_before = (owner[:, :, None] == owner[:, None, :]) & (
        order[None, None, :] < order[None, :, None]
    )
    rank = jnp.sum(same_before.astype(jnp.int32), axis=2)
    slot = owner * capacity + rank
    slot_ids = jnp.arange(slot_count)
    matched = slot[:, :, None] == slot_ids[None, None, :]
    request = jnp.sum(jnp.where(matched, local_row[:, :, None] + 1, 0), axis=1) - 1
    valid = request >= 0
    requested_in = lax.all_to_all(
        request.reshape(stream_count, seq_count, capacity),
        "seq",
        split_axis=1,
        concat_axis=1,
        tiled=True,
    )
    row_ids = jnp.maximum(requested_in, 0).reshape(stream_count, slot_count)
    mem_kv = fetch_rows(mem_keys, mem_values, row_ids, seq_count, capacity)
    key_pos = (part_pos - (BPS - 1)) * block_len + jnp.arange(seg_width)
    query_pos = part_pos * block_len + jnp.arange(block_len)
    local_ok = (
        (key_pos[None, None, :] >= 0)
        & (key_pos[None, None, :] <= query_pos[None, :, None])
        & (key_pos[None, None, :] < lengths[:, None, None])
    )
    memory_ok = jnp.broadcast_to(valid[:, None, :], (stream_count, block_len, slot_count))
    allowed = jnp.concatenate((local_ok, memory_ok), axis=2)
    query_blocks = queries.reshape(stream_count, block_len, attn_width)
    attended, log_total = lax.map(attend_forward, (query_blocks, kv_seg, mem_kv, allowed))
    attended_low = attended.astype(jnp.bfloat16).reshape(-1, attn_width)
    middle = tokens_f + jnp.dot(attended_low, w_out, preferred_element_type=jnp.float32)
    factor_two = rms_factor(middle)
    unit_two = middle * factor_two
    normed_two = (unit_two * gain_two).astype(jnp.bfloat16)
    gate = jnp.dot(normed_two, w_gate, preferred_element_type=jnp.float32)
    upper = jnp.dot(normed_two, w_up, preferred_element_type=jnp.float32)
    sigma = jax.nn.sigmoid(gate)
    hidden = (gate * sigma * upper).astype(jnp.bfloat16)
    layer_out = (middle + jnp.dot(hidden, w_down, preferred_element_type=jnp.float32)).astype(
        jnp.bfloat16
    )
    grad_y = cotangent.astype(jnp.float32).reshape(-1, model_width)
    grad_y_low = grad_y.astype(jnp.bfloat16)
    grad_down = jnp.einsum("nf,nd->fd", hidden, grad_y_low, preferred_element_type=jnp.float32)
    grad_hidden = jnp.einsum("nd,fd->nf", grad_y_low, w_down, preferred_element_type=jnp.float32)
    grad_gate_act = (grad_hidden * upper * sigma * (1.0 + gate * (1.0 - sigma))).astype(
        jnp.bfloat16
    )
    grad_up_act = (grad_hidden * gate * sigma).astype(jnp.bfloat16)
    grad_gate = jnp.einsum(
        "nd,nf->df", normed_two, grad_gate_act, preferred_element_type=jnp.float32
    )
    grad_up = jnp.einsum("nd,nf->df", normed_two, grad_up_act, preferred_element_type=jnp.float32)
    grad_normed_two = jnp.einsum(
        "nf,df->nd", grad_gate_act, w_gate, preferred_element_type=jnp.float32
    ) + jnp.einsum("nf,df->nd", grad_up_act, w_up, preferred_element_type=jnp.float32)
    grad_ffn_gain = jnp.sum(grad_normed_two * unit_two, axis=0)
    scaled_two = gain_two * grad_normed_two
    grad_middle = grad_y + factor_two * (
        scaled_two - unit_two * jnp.mean(scaled_two * unit_two, axis=-1, keepdims=True)
    )
    grad_branch = grad_middle.astype(jnp.bfloat16)
    grad_out = jnp.einsum(
        "nh,nd->hd", attended_low, grad_branch, preferred_element_type=jnp.float32
    )
    grad_attended = jnp.einsum(
        "nd,hd->nh", grad_branch, w_out, preferred_element_type=jnp.float32
    ).astype(jnp.bfloat16)
    kv_back = neighbour_blocks(kv_own)
    mem_back = fetch_rows(mem_keys, mem_values, row_ids, seq_count, capacity)
    grad_queries, grad_keys_all, grad_values_all = lax.map(
        attend_backward,
        (
            query_blocks,
            kv_back,
            mem_back,
            allowed,
            log_total,
            grad_attended.reshape(stream_count, block_len, attn_width),
        ),
    )
    grad_local = jnp.stack((grad_keys_all[:, :seg_width], grad_values_all[:, :seg_width]), axis=1)
    grad_memory = jnp.stack((grad_keys_all[:, seg_width:], grad_values_all[:, seg_width:]), axis=1)
    own_grad = grad_local[:, :, (BPS - 1) * block_len :]
    for distance in range(1, BPS):
        offset = (BPS - 1 - distance) * block_len
        piece = grad_local[:, :, offset : offset + block_len]
        own_grad = own_grad + from_behind(piece.astype(jnp.bfloat16), "seq", -distance).astype(
            piece.dtype
        )
    grad_memory = jnp.where(valid[:, None, :, None], grad_memory, 0.0)
    returned = lax.all_to_all(
        grad_memory.reshape(stack_shape(stream_count, seq_count, capacity, attn_width)).astype(
            jnp.bfloat16
        ),
        "seq",
        split_axis=2,
        concat_axis=2,
        tiled=True,
    ).astype(jnp.float32)
    returned = returned.reshape(stream_count, 2, slot_count, attn_width)
    empty_table = jnp.zeros((stream_count, mem_rows, attn_width), jnp.float32)
    grad_mem_keys = jax.vmap(add_rows)(empty_table, row_ids, returned[:, 0])
    grad_mem_values = jax.vmap(add_rows)(empty_table, row_ids, returned[:, 1])
    grad_q_low = grad_queries.astype(jnp.bfloat16).reshape(-1, attn_width)
    grad_k_low = own_grad[:, 0].astype(jnp.bfloat16).reshape(-1, attn_width)
    grad_v_low = own_grad[:, 1].astype(jnp.bfloat16).reshape(-1, attn_width)
    grad_query = jnp.einsum("nd,nh->dh", normed_one, grad_q_low, preferred_element_type=jnp.float32)
    grad_key = jnp.einsum("nd,nh->dh", normed_one, grad_k_low, preferred_element_type=jnp.float32)
    grad_value = jnp.einsum("nd,nh->dh", normed_one, grad_v_low, preferred_element_type=jnp.float32)
    grad_normed_one = (
        jnp.einsum("nh,dh->nd", grad_q_low, w_query, preferred_element_type=jnp.float32)
        + jnp.einsum("nh,dh->nd", grad_k_low, w_key, preferred_element_type=jnp.float32)
        + jnp.einsum("nh,dh->nd", grad_v_low, w_value, preferred_element_type=jnp.float32)
    )
    grad_attn_gain = jnp.sum(grad_normed_one * unit_one, axis=0)
    scaled_one = gain_one * grad_normed_one
    grad_input = grad_middle + factor_one * (
        scaled_one - unit_one * jnp.mean(scaled_one * unit_one, axis=-1, keepdims=True)
    )
    grad_tokens = grad_input.astype(jnp.bfloat16).reshape(stream_count, block_len, model_width)
    summed = (
        lax.psum_scatter(grad_query, ("seq", "doc"), scatter_dimension=0, tiled=True),
        lax.psum_scatter(grad_key, ("seq", "doc"), scatter_dimension=0, tiled=True),
        lax.psum_scatter(grad_value, ("seq", "doc"), scatter_dimension=0, tiled=True),
        lax.psum_scatter(grad_out, ("seq", "doc"), scatter_dimension=0, tiled=True),
        lax.psum_scatter(grad_attn_gain, ("seq", "doc"), scatter_dimension=0, tiled=True),
        lax.psum_scatter(grad_gate, ("seq", "doc"), scatter_dimension=0, tiled=True),
        lax.psum_scatter(grad_up, ("seq", "doc"), scatter_dimension=0, tiled=True),
        lax.psum_scatter(grad_down, ("seq", "doc"), scatter_dimension=0, tiled=True),
        lax.psum_scatter(grad_ffn_gain, ("seq", "doc"), scatter_dimension=0, tiled=True),
    )
    return (
        layer_out.reshape(stream_count, block_len, model_width),
        grad_tokens,
        summed[4],
        summed[0],
        summed[1],
        summed[2],
        summed[3],
        summed[8],
        summed[5],
        summed[6],
        summed[7],
        grad_mem_keys,
        grad_mem_values,
    )


def solution(mesh):
    in_specs = (
        P("doc", "seq", None),
        P("doc", "seq", None),
        P(),
        P(),
        P(),
        P(),
        P(),
        P(),
        P(),
        P(),
        P(),
        P("doc", "seq", None),
        P("doc", "seq", None),
        P("doc", None),
        P("doc", "seq", None),
    )
    out_specs = (
        P("doc", "seq", None),
        P("doc", "seq", None),
        P(("seq", "doc")),
        P(("seq", "doc"), None),
        P(("seq", "doc"), None),
        P(("seq", "doc"), None),
        P(("seq", "doc"), None),
        P(("seq", "doc")),
        P(("seq", "doc"), None),
        P(("seq", "doc"), None),
        P(("seq", "doc"), None),
        P("doc", "seq", None),
        P("doc", "seq", None),
    )
    return jax.shard_map(
        on_device, mesh=mesh, in_specs=in_specs, out_specs=out_specs, check_vma=False
    )
```

profile of v0, /device:TPU:0, one launch (start us, length us, event | category | flops | bytes accessed | tf_op | source)
XLA Modules:
  0.0 1666.1 jit_solution(14883458805642210141)
XLA Ops:
  41.5 71.2 %all-to-all-done = s32[1,8,32]{2,0,1:T(1,128)S(1)} async-done(((s32[1,8,32]{2,0,1:T(1,128)}), s32[1,8,32]{2,0,1:T(1,128)S(1)}, u32[]{:S(2)}, u32[]{:S(2)}) %all-to-all-start) | async-done | bytes 1056 | tf_op jit(solution)/shard_map/all_to_all | solution.py:168
  116.7 7.7 gather_fusion
  126.9 27.5 %all-to-all-start.1 = ((bf16[1,2,8,32,1024]{4,3,1,0,2:T(8,128)(2,1)}), bf16[1,2,8,32,1024]{4,3,1,0,2:T(8,128)(2,1)}, u32[]{:S(2)}, u32[]{:S(2)}) async-start(bf16[1,2,8,32,1024]{4,3,1,0,2:T(8,128)(2,1)} %pad_maximum_fusion.7), calls=%async_computation.1 | async-start | bytes 2097152 | tf_op jit(solution)/shard_map/all_to_all | solution.py:48
  156.2 13.8 all-to-all-done.1
  185.7 6.5 copy.101
  199.2 18.8 %fusion.78 = (f32[8,512]{1,0:T(8,128)S(1)}, f32[8,512,2304]{2,1,0:T(8,128)}) fusion(bf16[512,8,128]{0,2,1:T(8,128)(2,1)S(1)} %bitcast.202, bf16[2304,8,128]{2,0,1:T(8,128)(2,1)} %copy_dynamic-update-slice_fusion.1, pred[512,2304]{1,0:T(8,128)(4,1)} %add_bitcast_fusion), kind=kOutput, calls=%fused_computation.153 | convolution fusion | flops 2444226560 | bytes 44711936 | tf_op jit(solution)/shard_map/while/body/eval_jaxpr/qhd,khd->hqk/dot_general | solution.py:63
  217.9 17.6 %fusion = f32[8,512]{1,0:T(8,128)S(1)} fusion(f32[8,512,2304]{2,1,0:T(8,128)} %get-tuple-element.88, f32[8,512]{1,0:T(8,128)S(1)} %get-tuple-element.87), kind=kLoop, calls=%fused_computation.10 | loop fusion | flops 18870272 | bytes 37781504 | tf_op jit(solution)/shard_map/while/body/eval_jaxpr/reduce_sum | solution.py:74
  235.7 14.9 fusion.30
  252.3 19.8 %fusion.80 = f32[512,2816]{1,0:T(8,128)} fusion(bf16[512,1024]{1,0:T(8,128)(2,1)S(1)} %multiply_convert_fusion.5, bf16[1024,2816]{1,0:T(8,128)(2,1)} %param.26), kind=kOutput, calls=%fused_computation.155 | convolution fusion | flops 2952790016 | bytes 12582912 | tf_op jit(solution)/shard_map/dot_general | solution.py:194
  272.1 5.0 fusion.79
  277.2 11.8 multiply_convert_fusion.1
  289.0 5.1 fusion.81
  294.1 6.2 multiply_reduce_fusion.1
  308.8 26.7 %multiply_reduce_fusion = (f32[8,512]{1,0:T(8,128)S(1)}, f32[8,512,2304]{2,1,0:T(8,128)}) fusion(f32[8,512,2304]{2,1,0:T(8,128)} %get-tuple-element.88, f32[8,512]{1,0:T(8,128)S(1)} %log_add_fusion, bf16[512,8,128]{0,2,1:T(8,128)(2,1)} %bitcast.204, bf16[256,8,128]{0,2,1:T(8,128)(2,1)} %copy.86, bf16[2048,8,128]{0,2,1:T(8,128)(2,1)} %bitcast.199), kind=kOutput, calls=%fused_computation.5 | convolution fusion | flops 2453663744 | bytes 81297408 | tf_op jit(solution)/shard_map/while/body/eval_jaxpr/qhd,khd->hqk/dot_general | solution.py:85
  335.5 31.0 %multiply_convert_fusion = bf16[8,512,2304]{2,1,0:T(8,128)(2,1)} fusion(f32[8,512,2304]{2,1,0:T(8,128)} %get-tuple-element.93, f32[8,512,2304]{2,1,0:T(8,128)} %get-tuple-element.88, f32[8,512]{1,0:T(8,128)S(1)} %get-tuple-element.92, f32[8,512]{1,0:T(8,128)S(1)} %log_add_fusion), kind=kLoop, calls=%fused_computation.4 | loop fusion | flops 37748736 | bytes 94404608 | tf_op jit(solution)/shard_map/while/body/eval_jaxpr/convert_element_type | solution.py:89
  366.5 12.5 multiply_convert_fusion.4
  379.0 4.8 fusion.70
  383.9 19.9 %fusion.2 = f32[8,128,2304]{2,1,0:T(8,128)} fusion(bf16[512,8,128]{0,2,1:T(8,128)(2,1)} %bitcast.205, f32[8,512,2304]{2,1,0:T(8,128)} %get-tuple-element.88, f32[8,512]{1,0:T(8,128)S(1)} %log_add_fusion), kind=kOutput, calls=%fused_computation.15 | convolution fusion | flops 2434793472 | bytes 48250880 | tf_op jit(solution)/shard_map/while/body/eval_jaxpr/hqk,qhd->khd/dot_general | solution.py:97
  407.9 12.8 convolution_multiply_fusion
  438.6 51.3 %collective-permute-done.5 = bf16[1,2,512,1024]{2,3,1,0:T(8,128)(2,1)S(1)} collective-permute-done((bf16[1,2,512,1024]{2,3,1,0:T(8,128)(2,1)S(1)}, bf16[1,2,512,1024]{2,3,1,0:T(8,128)(2,1)S(1)}, u32[]{:S(2)}, u32[]{:S(2)}) %collective-permute-start.5) | collective-permute-done | bytes 2097184 | tf_op jit(solution)/shard_map/ppermute | solution.py:19
  489.9 48.7 %collective-permute-done.4 = bf16[1,2,512,1024]{2,3,1,0:T(8,128)(2,1)S(1)} collective-permute-done((bf16[1,2,512,1024]{2,3,1,0:T(8,128)(2,1)S(1)}, bf16[1,2,512,1024]{2,3,1,0:T(8,128)(2,1)S(1)}, u32[]{:S(2)}, u32[]{:S(2)}) %collective-permute-start.4) | collective-permute-done | bytes 2097184 | tf_op jit(solution)/shard_map/ppermute | solution.py:19
  549.9 9.7 fusion.84
  559.7 9.6 fusion.83
  569.3 9.5 fusion.40
  590.5 14.3 all-to-all-start.2
  609.4 6.7 fusion.33
  640.1 56.9 %all-reduce.2 = (f32[1024]{0:T(1024)S(1)}, f32[1024]{0:T(1024)S(1)}) all-reduce(f32[1024]{0:T(1024)S(1)} %get-tuple-element.57, f32[1024]{0:T(1024)S(1)} %copy-done.27), channel_id=2, replica_groups=mesh['seq'=8,'doc'=4] {'seq','doc'}, use_global_device_ids=true, to_apply=%region_10.12.clone | all-reduce | flops 2048 | bytes 16384
  701.8 52.9 %reduce-scatter.10.cloned.1.call-done = f32[32,1024]{1,0:T(8,128)} async-done(((f32[1024,1024]{1,0:T(8,128)}), f32[32,1024]{1,0:T(8,128)}) %reduce-scatter.10.cloned.1.call-update) | async-done | bytes 131088 | tf_op jit(solution)/shard_map/reduce_scatter | solution.py:282
  754.8 148.8 %reduce-scatter.12.cloned.1.call-done = f32[32,1024]{1,0:T(8,128)} async-done(((f32[1024,1024]{1,0:T(8,128)}), f32[32,1024]{1,0:T(8,128)}) %reduce-scatter.12.cloned.1.call-update) | async-done | bytes 131088 | tf_op jit(solution)/shard_map/reduce_scatter | solution.py:283
  903.5 253.0 %reduce-scatter.18.cloned.1.call-done = f32[32,2816]{1,0:T(8,128)} async-done(((f32[1024,2816]{1,0:T(8,128)}), f32[32,2816]{1,0:T(8,128)}) %reduce-scatter.18.cloned.1.call-update) | async-done | bytes 360464 | tf_op jit(solution)/shard_map/reduce_scatter | solution.py:287
  1156.5 251.2 %reduce-scatter.16.cloned.1.call-done = f32[32,2816]{1,0:T(8,128)} async-done(((f32[1024,2816]{1,0:T(8,128)}), f32[32,2816]{1,0:T(8,128)}) %reduce-scatter.16.cloned.1.call-update) | async-done | bytes 360464 | tf_op jit(solution)/shard_map/reduce_scatter | solution.py:286
  1407.7 251.3 %reduce-scatter.20.cloned.1.call-done = f32[88,1024]{1,0:T(8,128)} async-done(((f32[2816,1024]{1,0:T(8,128)}), f32[88,1024]{1,0:T(8,128)}) %reduce-scatter.20.cloned.1.call-update) | async-done | bytes 360464 | tf_op jit(solution)/shard_map/reduce_scatter | solution.py:288
  (185 shorter events, 153.4 us)
Async XLA Ops:
  8.9 26.4 %copy-start.24 = (f32[512]{0:T(512)}, f32[512]{0:T(512)S(1)}, u32[]{:S(2)}) copy-start(f32[512]{0:T(512)S(1)} %add_rsqrt_fusion.1) | copy-start | bytes 6148
  9.6 25.7 %copy-start.22 = (f32[1024]{0:T(1024)}, f32[1024]{0:T(1024)S(1)}, u32[]{:S(2)}) copy-start(f32[1024]{0:T(1024)S(1)} %convert_element_type.148) | copy-start | bytes 12292
  13.6 14.1 copy-start.32
  13.6 18.5 %copy-start.33 = (s32[1,2]{1,0:T(1,128)S(1)}, s32[1,2]{1,0:T(1,128)}, u32[]{:S(2)}) copy-start(s32[1,2]{1,0:T(1,128)} %param.30) | copy-start | bytes 28
  15.3 161.8 %collective-permute-start.2 = (bf16[1,2,512,1024]{3,2,1,0:T(8,128)(2,1)}, bf16[1,2,512,1024]{3,2,1,0:T(8,128)(2,1)}, u32[]{:S(2)}, u32[]{:S(2)}) collective-permute-start(bf16[1,2,512,1024]{3,2,1,0:T(8,128)(2,1)} %pad_maximum_fusion.4), channel_id=1, source_target_pairs={{0,4},{4,8},{8,12},{12,16},{16,20},{20,24},{24,28},{1,5},{5,9},{9,... | collective-permute-start | bytes 6291464 | tf_op jit(solution)/shard_map/ppermute | solution.py:19
  18.9 158.2 %collective-permute-start.1 = (bf16[1,2,512,1024]{3,2,1,0:T(8,128)(2,1)}, bf16[1,2,512,1024]{3,2,1,0:T(8,128)(2,1)}, u32[]{:S(2)}, u32[]{:S(2)}) collective-permute-start(bf16[1,2,512,1024]{3,2,1,0:T(8,128)(2,1)} %pad_maximum_fusion.4), channel_id=1, source_target_pairs={{0,8},{4,12},{8,16},{12,20},{16,24},{20,28},{1,9},{5,13},{9,17},{1... | collective-permute-start | bytes 6291464 | tf_op jit(solution)/shard_map/ppermute | solution.py:19
  23.4 153.8 %collective-permute-start = (bf16[1,2,512,1024]{3,2,1,0:T(8,128)(2,1)}, bf16[1,2,512,1024]{3,2,1,0:T(8,128)(2,1)}, u32[]{:S(2)}, u32[]{:S(2)}) collective-permute-start(bf16[1,2,512,1024]{3,2,1,0:T(8,128)(2,1)} %pad_maximum_fusion.4), channel_id=1, source_target_pairs={{0,12},{4,16},{8,20},{12,24},{16,28},{1,13},{5,17},{9,21},{13,25},... | collective-permute-start | bytes 6291464 | tf_op jit(solution)/shard_map/ppermute | solution.py:19
  28.7 84.0 %all-to-all-start = ((s32[1,8,32]{2,0,1:T(1,128)}), s32[1,8,32]{2,0,1:T(1,128)S(1)}, u32[]{:S(2)}, u32[]{:S(2)}) async-start(s32[1,8,32]{2,0,1:T(1,128)} %sub.69), calls=%async_computation | async-start | bytes 8192 | tf_op jit(solution)/shard_map/all_to_all | solution.py:168
  39.1 74.3 %copy-start.5 = (bf16[1,512,1024]{2,1,0:T(8,128)(2,1)S(1)}, bf16[1,512,1024]{2,1,0:T(8,128)(2,1)}, u32[]{:S(2)}) copy-start(bf16[1,512,1024]{2,1,0:T(8,128)(2,1)} %param.29) | copy-start | bytes 3145732
  124.4 30.2 %copy-start.12 = (pred[1,512,2048]{2,1,0:T(8,128)(4,1)S(1)}, pred[1,512,2048]{2,1,0:T(8,128)(4,1)}, u32[]{:S(2)}) copy-start(pred[1,512,2048]{2,1,0:T(8,128)(4,1)} %and_and_fusion) | copy-start | bytes 3145732
  126.9 43.1 %all-to-all-start.1 = ((bf16[1,2,8,32,1024]{4,3,1,0,2:T(8,128)(2,1)}), bf16[1,2,8,32,1024]{4,3,1,0,2:T(8,128)(2,1)}, u32[]{:S(2)}, u32[]{:S(2)}) async-start(bf16[1,2,8,32,1024]{4,3,1,0,2:T(8,128)(2,1)} %pad_maximum_fusion.7), calls=%async_computation.1 | async-start | bytes 2097152 | tf_op jit(solution)/shard_map/all_to_all | solution.py:48
  154.5 547.4 %reduce-scatter.14.cloned.1.call-start = ((), (), s32[]{:S(2)}) async-start(), calls=%async_computation.13 | async-start | bytes 4325376 | tf_op jit(solution)/shard_map/reduce_scatter | solution.py:284
  154.5 20.6 %copy-start.29 = (pred[256]{0:T(512)(128)(4,1)}, pred[256]{0:T(512)(128)(4,1)S(1)}, u32[]{:S(2)}) copy-start(pred[256]{0:T(512)(128)(4,1)S(1)} %broadcast_compare_fusion) | copy-start | bytes 772
  156.2 21.0 %copy-start.14 = (bf16[1,1,512,1024]{3,2,1,0:T(8,128)(2,1)S(1)}, bf16[1,1,512,1024]{3,2,1,0:T(8,128)(2,1)}, u32[]{:S(2)}) copy-start(bf16[1,1,512,1024]{3,2,1,0:T(8,128)(2,1)} %copy-done.13) | copy-start | bytes 3145732
  217.9 17.7 %copy-start.4 = (bf16[1,1,2048,1024]{2,3,1,0:T(8,128)(2,1)S(1)}, bf16[1,1,2048,1024]{2,3,1,0:T(8,128)(2,1)}, u32[]{:S(2)}) copy-start(bf16[1,1,2048,1024]{2,3,1,0:T(8,128)(2,1)} %copy.101) | copy-start | bytes 12582916
  217.9 17.7 %copy-start.16 = (bf16[256,8,128]{0,2,1:T(8,128)(2,1)S(1)}, bf16[256,8,128]{0,2,1:T(8,128)(2,1)}, u32[]{:S(2)}) copy-start(bf16[256,8,128]{0,2,1:T(8,128)(2,1)} %copy.86) | copy-start | bytes 1572868
  235.6 14.9 copy-start.7
  235.6 14.9 copy-start.17
  250.6 21.5 %slice-start = ((s8[5767168]{0:T(1024)(128)(4,1)}), s8[4194304]{0:T(1024)(128)(4,1)S(1)}, s32[]{:S(2)}) async-start(s8[5767168]{0:T(1024)(128)(4,1)} %bitcast.223), calls=%async_computation.17 | async-start | bytes 8388608
  252.0 48.4 %copy-start.2 = (f32[512,1024]{1,0:T(8,128)}, f32[512,1024]{1,0:T(8,128)S(1)}, u32[]{:S(2)}) copy-start(f32[512,1024]{1,0:T(8,128)S(1)} %get-tuple-element.90) | copy-start | bytes 6291460
  252.2 19.9 %copy-start.20 = (bf16[512,1024]{1,0:T(8,128)(2,1)}, bf16[512,1024]{1,0:T(8,128)(2,1)S(1)}, u32[]{:S(2)}) copy-start(bf16[512,1024]{1,0:T(8,128)(2,1)S(1)} %multiply_convert_fusion.5) | copy-start | bytes 3145732
  252.2 19.9 %slice-start.1 = ((s8[5767168]{0:T(1024)(128)(4,1)}), s8[1572864]{0:T(1024)(128)(4,1)S(1)}, s32[]{:S(2)}) async-start(s8[5767168]{0:T(1024)(128)(4,1)} %bitcast.223), calls=%async_computation.18 | async-start | bytes 3145728
  308.8 393.1 %reduce-scatter.8.cloned.1.call-start = ((), (), s32[]{:S(2)}) async-start(), calls=%async_computation.10 | async-start | bytes 4325376 | tf_op jit(solution)/shard_map/reduce_scatter | solution.py:281
  383.9 370.9 %reduce-scatter.10.cloned.1.call-start = ((), (), s32[]{:S(2)}) async-start(), calls=%async_computation.11 | async-start | bytes 4325376 | tf_op jit(solution)/shard_map/reduce_scatter | solution.py:282
  432.5 6.1 collective-permute-start.3
  433.8 56.0 %collective-permute-start.5 = (bf16[1,2,512,1024]{2,3,1,0:T(8,128)(2,1)S(1)}, bf16[1,2,512,1024]{2,3,1,0:T(8,128)(2,1)S(1)}, u32[]{:S(2)}, u32[]{:S(2)}) collective-permute-start(bf16[1,2,512,1024]{2,3,1,0:T(8,128)(2,1)S(1)} %get-tuple-element.75), channel_id=1, source_target_pairs={{12,0},{16,4},{20,8},{24,12},{28,16},{13,1},{17,5},{21,9},{25,13},... | collective-permute-start | bytes 6291464 | tf_op jit(solution)/shard_map/ppermute | solution.py:19
  435.1 103.5 %collective-permute-start.4 = (bf16[1,2,512,1024]{2,3,1,0:T(8,128)(2,1)S(1)}, bf16[1,2,512,1024]{2,3,1,0:T(8,128)(2,1)S(1)}, u32[]{:S(2)}, u32[]{:S(2)}) collective-permute-start(bf16[1,2,512,1024]{2,3,1,0:T(8,128)(2,1)S(1)} %get-tuple-element.76), channel_id=1, source_target_pairs={{8,0},{12,4},{16,8},{20,12},{24,16},{28,20},{9,1},{13,5},{17,9},{2... | collective-permute-start | bytes 6291464 | tf_op jit(solution)/shard_map/ppermute | solution.py:19
  545.0 358.6 %reduce-scatter.12.cloned.1.call-start = ((), (), s32[]{:S(2)}) async-start(), calls=%async_computation.12 | async-start | bytes 4325376 | tf_op jit(solution)/shard_map/reduce_scatter | solution.py:283
  549.7 606.8 %reduce-scatter.18.cloned.1.call-start = ((), (), s32[]{:S(2)}) async-start(), calls=%async_computation.15 | async-start | bytes 11894784 | tf_op jit(solution)/shard_map/reduce_scatter | solution.py:287
  559.6 848.1 %reduce-scatter.16.cloned.1.call-start = ((), (), s32[]{:S(2)}) async-start(), calls=%async_computation.14 | async-start | bytes 11894784 | tf_op jit(solution)/shard_map/reduce_scatter | solution.py:286
  569.3 1089.8 %reduce-scatter.20.cloned.1.call-start = ((), (), s32[]{:S(2)}) async-start(), calls=%async_computation.16 | async-start | bytes 11894784 | tf_op jit(solution)/shard_map/reduce_scatter | solution.py:288
  590.5 30.6 %all-to-all-start.2 = ((bf16[1,2,8,32,1024]{4,3,1,0,2:T(8,128)(2,1)}), bf16[1,2,8,32,1024]{4,3,1,0,2:T(8,128)(2,1)}, u32[]{:S(2)}, u32[]{:S(2)}) async-start(bf16[1,2,8,32,1024]{4,3,1,0,2:T(8,128)(2,1)} %copy.97), calls=%async_computation.9 | async-start | bytes 2097152 | tf_op jit(solution)/shard_map/all_to_all | solution.py:250
  (22 other events, 84.7 us)
Sparse Core Ops, SparseCore 0:
  308.9 145.4 reduce-scatter.13
  457.3 147.0 reduce-scatter.7
  607.2 147.4 reduce-scatter.9
  757.5 146.0 reduce-scatter.11
  906.3 250.1 reduce-scatter.17
  1159.2 248.4 reduce-scatter.15
  1410.6 248.4 reduce-scatter.19
where the time goes:
time: 1670 us
  waiting for transfers between devices  1150 us (69%)
  matrix products  228 us (14%)
  other arithmetic  87.7 us (5%)
  local copies, waits for them, and re-layouts  67.4 us (4%)
  starting transfers between devices  61.9 us (4%)
  blocking collectives  56.9 us (3%)
    reduce_scatter x1, waiting for transfers between devices, on_device(): lax.psum_scatter(grad_up, ('seq', 'doc'), scatter_dimension=0, tiled=True)  253 us
    reduce_scatter x1, waiting for transfers between devices, on_device(): lax.psum_scatter(grad_down, ('seq', 'doc'), scatter_dimension=0, tiled=True)  251 us
    reduce_scatter x1, waiting for transfers between devices, on_device(): lax.psum_scatter(grad_gate, ('seq', 'doc'), scatter_dimension=0, tiled=True)  251 us
    reduce_scatter x1, waiting for transfers between devices, on_device(): lax.psum_scatter(grad_value, ('seq', 'doc'), scatter_dimension=0, tiled=T...  149 us
    ppermute x6, waiting for transfers between devices, from_behind(): lax.ppermute(value, axis, [(source, source + steps) for source in range(l...  102 us
    all_to_all x1, waiting for transfers between devices, on_device(): lax.all_to_all(request.reshape(stream_count, seq_count, capacity), 'seq',...  71.2 us
    unnamed x1, blocking collectives  56.9 us
    reduce_scatter x1, waiting for transfers between devices, on_device(): lax.psum_scatter(grad_key, ('seq', 'doc'), scatter_dimension=0, tiled=True)  52.9 us
  transfers between devices with their start and end apart: 16, of which 11 were waited for; matrix products, arithmetic and copies ran while one was open for 14% of the time, Pallas kernels for 0%

commit v1 on v0

--- a/solution.py
+++ b/solution.py
@@ -1,6 +1,8 @@
 import jax
 import jax.numpy as jnp
 from jax import lax
+from jax.experimental import pallas as pl
+from jax.experimental.pallas import tpu as pltpu
 from jax.sharding import PartitionSpec as P
 
 HEADS = 8
@@ -102,6 +104,217 @@
         grad_queries.reshape(queries.shape[0], attn_width),
         grad_keys.reshape(-1, attn_width),
         grad_values.reshape(-1, attn_width),
+    )
+
+
+MESH = pl.DeviceIdType.MESH
+UNIT = 256
+SKEW = 2
+
+def flip(value, bit):
+    return value + bit - 2 * bit * ((value // bit) % 2)
+
+
+def partners():
+    seq, doc = lax.axis_index("seq"), lax.axis_index("doc")
+    return {
+        "core": (flip(seq, 1), doc),
+        "x": (flip(seq, 2), doc),
+        "y": (flip(seq, 4), doc),
+        "low": (seq, flip(doc, 1)),
+        "high": (seq, flip(doc, 2)),
+    }
+
+
+ORDERS = (("x", "y", "low", "high"), ("y", "x", "low", "high"), ("low", "high", "x", "y"))
+
+
+def rs_kernel(plan, every, names, refs_in, gains_in, refs_out, gains_out, own, stages, gain_buf, sems):
+    seq, doc = lax.axis_index("seq"), lax.axis_index("doc")
+    bits = {
+        "core": seq % 2,
+        "x": (seq // 2) % 2,
+        "y": (seq // 4) % 2,
+        "low": doc % 2,
+        "high": (doc // 2) % 2,
+    }
+    peer = partners()
+    local_sem, send_sem, recv_sem, gain_send, gain_recv = sems
+    barrier = pltpu.get_barrier_semaphore()
+    for name in ("core", "x", "y", "low", "high"):
+        pl.semaphore_signal(barrier, inc=1, device_id=peer[name], device_id_type=MESH)
+    pl.semaphore_wait(barrier, 5)
+
+    def pick(cls, level, unit, side):
+        order = ORDERS[cls]
+        ref = stages[cls][level]
+        name = order[level]
+        where = (1 - bits[name]) if side == "send" else bits[name]
+        left = [axis for axis in ("y", "x", "high", "low") if axis not in order[:level]]
+        index = (unit,) + (slice(None),) * left.index(name) + (where,)
+        return ref, index
+
+    def first(cls, unit, array, column):
+        source = refs_in[array]
+        lanes = pl.ds(column, UNIT)
+        there = source.at[:, :, 1 - bits["core"], :, :, :, lanes]
+        here = source.at[:, :, bits["core"], :, :, :, lanes]
+        local = pltpu.make_async_copy(here, own[cls].at[unit], local_sem[cls].at[unit])
+        remote = pltpu.make_async_remote_copy(
+            src_ref=there, dst_ref=stages[cls][0].at[unit],
+            send_sem=send_sem[cls].at[0, unit], recv_sem=recv_sem[cls].at[0, unit],
+            device_id=peer["core"], device_id_type=MESH)
+        return local, remote
+
+    def later(cls, level, unit):
+        ref, index = pick(cls, level - 1, unit, "send")
+        return pltpu.make_async_remote_copy(
+            src_ref=ref.at[index], dst_ref=stages[cls][level].at[unit],
+            send_sem=send_sem[cls].at[level, unit], recv_sem=recv_sem[cls].at[level, unit],
+            device_id=peer[ORDERS[cls][level - 1]], device_id_type=MESH)
+
+    def gain_copy(level):
+        name = ("core", "x", "y", "low", "high")[level]
+        return pltpu.make_async_remote_copy(
+            src_ref=gain_buf.at[0, level], dst_ref=gain_buf.at[1, level],
+            send_sem=gain_send.at[level], recv_sem=gain_recv.at[level],
+            device_id=peer[name], device_id_type=MESH)
+
+    gain_buf[0, 0] = gains_in[...]
+    gain_copy(0).start()
+    longest = max(len(units) * every[c] for c, units in enumerate(plan))
+    for step in range(longest):
+        for cls, units in enumerate(plan):
+            if step % every[cls] == 0 and step // every[cls] < len(units):
+                array, column = units[step // every[cls]]
+                local, remote = first(cls, step // every[cls], array, column)
+                remote.start()
+                local.start()
+
+    def arrive(cls, level, unit):
+        array, column = plan[cls][0]
+        ref = stages[cls][level]
+        if level == 0:
+            local, remote = first(cls, unit, array, column)
+            remote.wait_recv()
+            local.wait()
+            ref[unit] = ref[unit] + own[cls][unit]
+        else:
+            later(cls, level, unit).wait_recv()
+            prev, index = pick(cls, level - 1, unit, "keep")
+            if level < 4:
+                ref[unit] = ref[unit] + prev[index]
+            else:
+                refs_out[cls][unit] = ref[unit].astype(jnp.float32) + prev[index].astype(jnp.float32)
+        if level < 4:
+            later(cls, level + 1, unit).start()
+
+    def body(step, carry):
+        for level in range(4, -1, -1):
+            for cls, units in enumerate(plan):
+                at = step - level * SKEW
+                unit = at // every[cls]
+                ok = (at >= 0) & (unit < len(units))
+                if every[cls] > 1:
+                    ok = ok & (at % every[cls] == 0)
+
+                @pl.when(ok)
+                def _():
+                    arrive(cls, level, unit)
+        for level in range(5):
+            @pl.when(step == 3 * level + 2)
+            def _():
+                gain_copy(level).wait_recv()
+                total = gain_buf[0, level] + gain_buf[1, level]
+                if level < 4:
+                    gain_buf[0, level + 1] = total
+                    gain_copy(level + 1).start()
+                else:
+                    gains_out[...] = total
+        return carry
+
+    steps = max(longest, 15 - 4 * SKEW) + 4 * SKEW
+    lax.fori_loop(0, steps, body, 0)
+    for level in range(5):
+        gain_copy(level).wait_send()
+    for cls, units in enumerate(plan):
+        def drain(unit, carry):
+            first(cls, unit, *plan[cls][0])[1].wait_send()
+            for level in range(1, 5):
+                later(cls, level, unit).wait_send()
+            return carry
+        lax.fori_loop(0, len(units), drain, 0)
+
+
+def make_rs(plan, every, n_in):
+    rows = (32, 32, 88)
+    n = [len(p) for p in plan]
+    def shapes(cls):
+        u, r = n[cls], rows[cls]
+        return [(u,) + (2,) * k + (r, UNIT) for k in (4, 3, 2, 1, 0)]
+
+    def kernel(*refs):
+        refs_in = refs[:n_in]
+        gains_in = refs[n_in]
+        refs_out = refs[n_in + 1 : n_in + 4]
+        gains_out = refs[n_in + 4]
+        k = n_in + 5
+        own = refs[k : k + 3]
+        k += 3
+        stages = [refs[k + 5 * c : k + 5 * c + 5] for c in range(3)]
+        k += 15
+        gain_buf = refs[k]
+        k += 1
+        sems = (refs[k : k + 3], refs[k + 3 : k + 6], refs[k + 6 : k + 9], refs[k + 9], refs[k + 10])
+        rs_kernel(plan, every, None, refs_in, gains_in, refs_out, gains_out, own, stages, gain_buf, sems)
+
+    scratch = [pltpu.VMEM(shapes(c)[0], jnp.bfloat16) for c in range(3)]
+    for c in range(3):
+        scratch += [pltpu.VMEM(s, jnp.bfloat16) for s in shapes(c)]
+    scratch.append(pltpu.VMEM((2, 5, 16, 128), jnp.float32))
+    scratch += [pltpu.SemaphoreType.DMA((n[c],)) for c in range(3)]
+    scratch += [pltpu.SemaphoreType.DMA((5, n[c])) for c in range(3)]
+    scratch += [pltpu.SemaphoreType.DMA((5, n[c])) for c in range(3)]
+    scratch += [pltpu.SemaphoreType.DMA((5,)), pltpu.SemaphoreType.DMA((5,))]
+    return pl.pallas_call(
+        kernel,
+        out_shape=tuple(jax.ShapeDtypeStruct((n[c], rows[c], UNIT), jnp.float32) for c in range(3))
+        + (jax.ShapeDtypeStruct((16, 128), jnp.float32),),
+        in_specs=[pl.BlockSpec(memory_space=pl.ANY)] * n_in + [pl.BlockSpec(memory_space=pltpu.VMEM)],
+        out_specs=tuple(pl.BlockSpec(memory_space=pltpu.VMEM) for _ in range(4)),
+        scratch_shapes=scratch,
+        name="weight_sums",
+        compiler_params=pltpu.CompilerParams(collective_id=0, has_side_effects=True, vmem_limit_bytes=58 * 2**20),
+    )
+
+
+def weight_plan():
+    a = [(0, 256 * i) for i in range(11)] + [(2, 256 * i) for i in range(4)] + [(3, 256 * i) for i in range(4)]
+    b = [(1, 256 * i) for i in range(11)] + [(4, 256 * i) for i in range(4)] + [(5, 256 * i) for i in range(4)]
+    c = [(6, 256 * i) for i in range(4)]
+    return (a, b, c), (1, 1, 4)
+
+
+def reduce_weights(gate, up, query, key, value, out, down, gain_one, gain_two):
+    plan, every = weight_plan()
+    def wide(g):
+        return g.reshape(2, 2, 2, 2, 2, g.shape[0] // 32, g.shape[1])
+    gains = jnp.concatenate((gain_one, gain_two)).reshape(16, 128)
+    ins = [wide(gate), wide(up), wide(query), wide(key), wide(value), wide(out), wide(down), gains]
+    a, b, c, gsum = make_rs(plan, every, 7)(*ins)
+    def cols(x):
+        return x.transpose(1, 0, 2).reshape(x.shape[1], -1)
+    index = lax.axis_index("seq") * lax.axis_size("doc") + lax.axis_index("doc")
+    gsum = gsum.reshape(2, 32, 32)
+    mine = lax.dynamic_index_in_dim(gsum, index, 1, keepdims=False)
+    return (cols(a[:11]), cols(b[:11]), cols(a[11:15]), cols(a[15:19]), cols(b[11:15]), cols(b[15:19]), cols(c), mine[0], mine[1])
+
+def sum_weights(weights, gains):
+    if (lax.axis_size("seq"), lax.axis_size("doc")) == (8, 4):
+        return reduce_weights(*[grad.astype(jnp.bfloat16) for grad in weights], *gains)
+    return tuple(
+        lax.psum_scatter(grad, ("seq", "doc"), scatter_dimension=0, tiled=True)
+        for grad in weights + gains
     )
 
 
@@ -277,29 +490,22 @@
         scaled_one - unit_one * jnp.mean(scaled_one * unit_one, axis=-1, keepdims=True)
     )
     grad_tokens = grad_input.astype(jnp.bfloat16).reshape(stream_count, block_len, model_width)
-    summed = (
-        lax.psum_scatter(grad_query, ("seq", "doc"), scatter_dimension=0, tiled=True),
-        lax.psum_scatter(grad_key, ("seq", "doc"), scatter_dimension=0, tiled=True),
-        lax.psum_scatter(grad_value, ("seq", "doc"), scatter_dimension=0, tiled=True),
-        lax.psum_scatter(grad_out, ("seq", "doc"), scatter_dimension=0, tiled=True),
-        lax.psum_scatter(grad_attn_gain, ("seq", "doc"), scatter_dimension=0, tiled=True),
-        lax.psum_scatter(grad_gate, ("seq", "doc"), scatter_dimension=0, tiled=True),
-        lax.psum_scatter(grad_up, ("seq", "doc"), scatter_dimension=0, tiled=True),
-        lax.psum_scatter(grad_down, ("seq", "doc"), scatter_dimension=0, tiled=True),
-        lax.psum_scatter(grad_ffn_gain, ("seq", "doc"), scatter_dimension=0, tiled=True),
+    summed = sum_weights(
+        (grad_gate, grad_up, grad_query, grad_key, grad_value, grad_out, grad_down),
+        (grad_attn_gain, grad_ffn_gain),
     )
     return (
         layer_out.reshape(stream_count, block_len, model_width),
         grad_tokens,
+        summed[7],
+        summed[2],
+        summed[3],
         summed[4],
+        summed[5],
+        summed[8],
         summed[0],
         summed[1],
-        summed[2],
-        summed[3],
-        summed[8],
-        summed[5],
         summed[6],
-        summed[7],
         grad_mem_keys,
         grad_mem_values,
     )

time: 1670 us -> 726 us (0.43)
  waiting for transfers between devices: 1150 us -> 152 us
  Pallas kernels: 0 us -> 139 us
  blocking collectives: 56.9 us -> 0 us
  matrix products: 228 us -> 197 us
    reduce_scatter x7 -> x0, waiting for transfers between devices: 957 us -> none  [the longest x1 253 us: on_device(): lax.psum_scatter(grad_up, ('seq', 'doc'), scatter_dimension=0, tiled=True)]
    pallas_call x0 -> x1, Pallas kernels: none -> 139 us  [reduce_weights(): a, b, c, gsum = make_rs(plan, every, 7)(*ins)]
    ppermute x6, waiting for transfers between devices: 102 us -> 0.02 us  [from_behind(): lax.ppermute(value, axis, [(source, source + steps) for source in range(l...]
    all_to_all x1, waiting for transfers between devices: 4.83 us -> 68 us  [on_device(): lax.all_to_all(grad_memory.reshape(stack_shape(stream_count, seq_count, c...]
    unnamed x1 -> x0, blocking collectives: 56.9 us -> none
  transfers between devices with their start and end apart: 16 -> 9, of which waited for: 11 -> 3; matrix products, arithmetic and copies ran while one was open for 14% -> 10% of each run, Pallas kernels for 0% -> 0%
where the time goes in v1:
time: 726 us; the launch traced here: 717 us
  matrix products  197 us (27%)
  waiting for transfers between devices  152 us (21%)
  Pallas kernels  139 us (19%)
  other arithmetic  91.1 us (13%)
  local copies, waits for them, and re-layouts  80.9 us (11%)
  starting transfers between devices  55.6 us (8%)
    pallas_call x1, Pallas kernels, reduce_weights(): a, b, c, gsum = make_rs(plan, every, 7)(*ins)  139 us
    all_to_all x1, waiting for transfers between devices, on_device(): lax.all_to_all(request.reshape(stream_count, seq_count, capacity), 'seq',...  70.6 us
    all_to_all x1, waiting for transfers between devices, on_device(): lax.all_to_all(grad_memory.reshape(stack_shape(stream_count, seq_count, c...  68 us
    convert_element_type x1, other arithmetic, attend_backward(): grad_scores = (weights * (grad_weights - inner)).astype(jnp.bfloat16)  31 us
    dot_general x1, matrix products, attend_backward(): jnp.einsum('qhd,khd->hqk', grad_heads, vheads, preferred_element_type=jnp...  26.7 us
    all_to_all x1, starting transfers between devices, fetch_rows(): lax.all_to_all(stacked, 'seq', split_axis=2, concat_axis=2, tiled=True)  26.3 us
    dot_general x1, matrix products, attend_backward(): jnp.einsum('hqk,qhd->khd', weights.astype(jnp.bfloat16), grad_heads, pref...  18.9 us
    dot_general x1, matrix products, attention_scores(): jnp.einsum('qhd,khd->hqk', qheads, kheads, preferred_element_type=jnp.flo...  18.7 us
  transfers between devices with their start and end apart: 9, of which 3 were waited for; matrix products, arithmetic and copies ran while one was open for 10% of the time, Pallas kernels for 0%

profile of v1, /device:TPU:0, one launch (start us, length us, event | category | flops | bytes accessed | tf_op | source)
XLA Modules:
  0.0 717.3 jit_solution(1781649091625244350)
XLA Ops:
  12.5 4.4 collective-permute-start.1
  16.9 4.4 collective-permute-start
  35.6 70.6 %all-to-all-done = s32[1,8,32]{2,0,1:T(1,128)S(1)} async-done(((s32[1,8,32]{2,0,1:T(1,128)}), s32[1,8,32]{2,0,1:T(1,128)S(1)}, u32[]{:S(2)}, u32[]{:S(2)}) %all-to-all-start) | async-done | bytes 1056 | tf_op jit(solution)/shard_map/all_to_all | solution.py:381
  109.6 7.8 %gather_fusion.1 = bf16[256,1024]{1,0:T(8,128)(2,1)} fusion(bf16[1,512,1024]{2,1,0:T(8,128)(2,1)} %param.29, s32[256]{0:T(256)S(1)} %bitcast.234), kind=kCustom, calls=%fused_computation.1.clone | custom fusion | bytes 1050624 | tf_op jit(solution)/shard_map/vmap(jit(_take))/gather | solution.py:37
  119.9 26.3 %all-to-all-start.1 = ((bf16[1,2,8,32,1024]{4,3,1,0,2:T(8,128)(2,1)}), bf16[1,2,8,32,1024]{4,3,1,0,2:T(8,128)(2,1)}, u32[]{:S(2)}, u32[]{:S(2)}) async-start(bf16[1,2,8,32,1024]{4,3,1,0,2:T(8,128)(2,1)} %pad_maximum_fusion.7), calls=%async_computation.1 | async-start | bytes 2097152 | tf_op jit(solution)/shard_map/all_to_all | solution.py:50
  148.5 13.2 %all-to-all-done.1 = bf16[1,2,8,32,1024]{4,3,1,0,2:T(8,128)(2,1)} async-done(((bf16[1,2,8,32,1024]{4,3,1,0,2:T(8,128)(2,1)}), bf16[1,2,8,32,1024]{4,3,1,0,2:T(8,128)(2,1)}, u32[]{:S(2)}, u32[]{:S(2)}) %all-to-all-start.1) | async-done | bytes 1048608 | tf_op jit(solution)/shard_map/all_to_all | solution.py:50
  166.9 4.3 maximum_maximum_fusion
  177.8 6.6 copy.129
  186.3 18.7 %fusion.75 = (f32[8,512]{1,0:T(8,128)S(1)}, f32[8,512,2304]{2,1,0:T(8,128)}) fusion(bf16[512,8,128]{0,2,1:T(8,128)(2,1)S(1)} %bitcast.244, bf16[2304,8,128]{2,0,1:T(8,128)(2,1)} %copy_dynamic-update-slice_fusion.1, pred[512,2304]{1,0:T(8,128)(4,1)} %add_bitcast_fusion), kind=kOutput, calls=%fused_computation.166 | convolution fusion | flops 2444226560 | bytes 44711936 | tf_op jit(solution)/shard_map/while/body/eval_jaxpr/qhd,khd->hqk/dot_general | solution.py:65
  205.1 17.6 %fusion = f32[8,512]{1,0:T(8,128)S(1)} fusion(f32[8,512,2304]{2,1,0:T(8,128)} %get-tuple-element.100, f32[8,512]{1,0:T(8,128)S(1)} %get-tuple-element.99), kind=kLoop, calls=%fused_computation.10 | loop fusion | flops 18870272 | bytes 37781504 | tf_op jit(solution)/shard_map/while/body/eval_jaxpr/reduce_sum | solution.py:76
  222.8 15.1 %fusion.30 = bf16[8,128,512]{2,1,0:T(8,128)(2,1)S(1)} fusion(f32[8,512,2304]{2,1,0:T(8,128)} %get-tuple-element.100, f32[8,512]{1,0:T(8,128)S(1)} %fusion, f32[8,512]{1,0:T(8,128)S(1)} %get-tuple-element.99, bf16[256,8,128]{0,2,1:T(8,128)(2,1)S(1)} %copy-done.20, bf16[2048,8,128]{0,2,1:T(8,128)(2,1)S(1)} %bitcast.242), kind=kOutput, calls=%fused_computation.81 | convolution fusion | flops 2454192128 | bytes 43548672 | tf_op jit(solution)/shard_map/while/body/eval_jaxpr/hqk,khd->qhd/dot_general | solution.py:78
  239.6 8.7 %fusion.76 = f32[512,2816]{1,0:T(8,128)} fusion(bf16[512,1024]{1,0:T(8,128)(2,1)S(1)} %multiply_convert_fusion.5, bf16[1024,2816]{1,0:T(8,128)(2,1)} %param.25), kind=kOutput, calls=%fused_computation.167 | convolution fusion | flops 2952790016 | bytes 12582912 | tf_op jit(solution)/shard_map/dot_general | solution.py:406
  248.3 5.0 fusion.77
  253.3 11.5 %multiply_convert_fusion.1 = (bf16[512,2816]{1,0:T(8,128)(2,1)S(1)}, bf16[512,2816]{1,0:T(8,128)(2,1)}, bf16[512,2816]{1,0:T(8,128)(2,1)}) fusion(f32[512,2816]{1,0:T(8,128)} %fusion.76, f32[512,2816]{1,0:T(8,128)} %fusion.77, bf16[2816,1024]{1,0:T(8,128)(2,1)} %param.27, bf16[1,512,1024]{2,1,0:T(8,128)(2,1)S(1)} %copy-done.25), kind=kOutput, calls=%fused_computation.23 | convolution fusion | flops 2975858688 | bytes 27000832 | tf_op jit(solution)/shard_map/nd,fd->nf/dot_general | solution.py:416
  264.9 6.0 fusion.78
  270.9 6.2 multiply_reduce_fusion.1
  282.8 26.7 %multiply_reduce_fusion = (f32[8,512]{1,0:T(8,128)S(1)}, f32[8,512,2304]{2,1,0:T(8,128)}) fusion(f32[8,512,2304]{2,1,0:T(8,128)} %get-tuple-element.100, f32[8,512]{1,0:T(8,128)S(1)} %log_add_fusion, bf16[512,8,128]{0,2,1:T(8,128)(2,1)S(1)} %bitcast.246, bf16[256,8,128]{0,2,1:T(8,128)(2,1)} %copy.107, bf16[2048,8,128]{0,2,1:T(8,128)(2,1)} %bitcast.241), kind=kOutput, calls=%fused_computation.5 | convolution fusion | flops 2453663744 | bytes 81297408 | tf_op jit(solution)/shard_map/while/body/eval_jaxpr/qhd,khd->hqk/dot_general | solution.py:87
  309.6 18.9 %fusion.2 = f32[8,128,2304]{2,1,0:T(8,128)} fusion(bf16[512,8,128]{0,2,1:T(8,128)(2,1)S(1)} %bitcast.247, f32[8,512,2304]{2,1,0:T(8,128)} %get-tuple-element.100, f32[8,512]{1,0:T(8,128)S(1)} %log_add_fusion), kind=kOutput, calls=%fused_computation.15 | convolution fusion | flops 2434793472 | bytes 48250880 | tf_op jit(solution)/shard_map/while/body/eval_jaxpr/hqk,qhd->khd/dot_general | solution.py:99
  328.4 31.0 %multiply_convert_fusion = bf16[8,512,2304]{2,1,0:T(8,128)(2,1)} fusion(f32[8,512,2304]{2,1,0:T(8,128)} %get-tuple-element.105, f32[8,512,2304]{2,1,0:T(8,128)} %get-tuple-element.100, f32[8,512]{1,0:T(8,128)S(1)} %get-tuple-element.104, f32[8,512]{1,0:T(8,128)S(1)} %log_add_fusion), kind=kLoop, calls=%fused_computation.4 | loop fusion | flops 37748736 | bytes 94404608 | tf_op jit(solution)/shard_map/while/body/eval_jaxpr/convert_element_type | solution.py:91
  359.4 12.7 %convolution_multiply_fusion = f32[8,128,2304]{2,1,0:T(8,128)} fusion(bf16[512,8,128]{0,2,1:T(8,128)(2,1)S(1)} %bitcast.245, bf16[8,512,2304]{2,1,0:T(8,128)(2,1)} %multiply_convert_fusion), kind=kOutput, calls=%fused_computation.22 | convolution fusion | flops 2418278400 | bytes 29360128 | tf_op jit(solution)/shard_map/while/body/eval_jaxpr/hqk,qhd->khd/dot_general | solution.py:97
  372.1 11.8 %multiply_convert_fusion.4 = bf16[8,128,512]{2,1,0:T(8,128)(2,1)S(1)} fusion(bf16[2304,8,128]{2,0,1:T(8,128)(2,1)} %copy_dynamic-update-slice_fusion.1, bf16[8,512,2304]{2,1,0:T(8,128)(2,1)} %multiply_convert_fusion), kind=kOutput, calls=%fused_computation.66 | convolution fusion | flops 2416967680 | bytes 24641536 | tf_op jit(solution)/shard_map/while/body/eval_jaxpr/hqk,khd->qhd/dot_general | solution.py:94
  383.9 8.3 %convolution_convert_fusion.2 = bf16[1024,2816]{1,0:T(8,128)(2,1)} fusion(bf16[512,1024]{1,0:T(8,128)(2,1)} %copy-done.23, bf16[512,2816]{1,0:T(8,128)(2,1)} %get-tuple-element.78), kind=kOutput, calls=%fused_computation.29 | convolution fusion | flops 2955673600 | bytes 9699328 | tf_op jit(solution)/shard_map/nd,nf->df/dot_general | solution.py:421
  392.2 5.1 convolution_convert_fusion.1
  402.1 6.2 slice_bitcast_fusion.1
  415.9 5.8 fusion.72
  435.0 9.6 %all-to-all-start.2 = ((bf16[1,2,8,32,1024]{4,3,1,0,2:T(8,128)(2,1)}), bf16[1,2,8,32,1024]{4,3,1,0,2:T(8,128)(2,1)}, u32[]{:S(2)}, u32[]{:S(2)}) async-start(bf16[1,2,8,32,1024]{4,3,1,0,2:T(8,128)(2,1)} %copy.125), calls=%async_computation.2 | async-start | bytes 2097152 | tf_op jit(solution)/shard_map/all_to_all | solution.py:463
  448.8 7.0 convolution_convert_fusion
  460.0 68.0 %all-to-all-done.2 = bf16[1,2,8,32,1024]{4,3,1,0,2:T(8,128)(2,1)} async-done(((bf16[1,2,8,32,1024]{4,3,1,0,2:T(8,128)(2,1)}), bf16[1,2,8,32,1024]{4,3,1,0,2:T(8,128)(2,1)}, u32[]{:S(2)}, u32[]{:S(2)}) %all-to-all-start.2) | async-done | bytes 1048608 | tf_op jit(solution)/shard_map/all_to_all | solution.py:463
  531.0 4.8 scatter_custom_fusion
  535.7 4.8 scatter_custom_fusion.1
  540.5 5.0 fusion.10
  556.2 139.5 %weight_sums.1 = (f32[19,32,256]{2,1,0:T(8,128)}, f32[19,32,256]{2,1,0:T(8,128)}, f32[4,88,256]{2,1,0:T(8,128)}, f32[16,128]{1,0:T(8,128)}) custom-call(bf16[2,2,2,2,2,32,2816]{6,5,4,3,2,1,0:T(8,128)(2,1)} %bitcast.248, bf16[2,2,2,2,2,32,2816]{6,5,4,3,2,1,0:T(8,128)(2,1)} %bitcast.249, bf16[2,2,2,2,2,32,1024]{6,5,4,3,2,1,0:T(8,128)(2,1)} %bitcast.254, ...), custom_call_target="tpu_custom_call" | custom-call | tf_op jit(solution)/shard_map/weight_sums/pallas_call | solution.py:304
  (209 shorter events, 124.0 us)
Async XLA Ops:
  1.5 24.1 %copy-start.29 = (f32[1024]{0:T(1024)}, f32[1024]{0:T(1024)S(1)}, u32[]{:S(2)}) copy-start(f32[1024]{0:T(1024)S(1)} %convert_element_type.169) | copy-start | bytes 12292
  3.0 22.6 %copy-start.31 = (f32[512]{0:T(512)}, f32[512]{0:T(512)S(1)}, u32[]{:S(2)}) copy-start(f32[512]{0:T(512)S(1)} %add_rsqrt_fusion.1) | copy-start | bytes 6148
  7.1 14.1 %copy-start.39 = (s32[1,1,128]{2,1,0:T(1,128)S(1)}, s32[1,1,128]{2,1,0:T(1,128)}, u32[]{:S(2)}) copy-start(s32[1,1,128]{2,1,0:T(1,128)} %param.31) | copy-start | bytes 1540
  8.8 158.1 %collective-permute-start.2 = (bf16[1,2,512,1024]{3,2,1,0:T(8,128)(2,1)}, bf16[1,2,512,1024]{3,2,1,0:T(8,128)(2,1)}, u32[]{:S(2)}, u32[]{:S(2)}) collective-permute-start(bf16[1,2,512,1024]{3,2,1,0:T(8,128)(2,1)} %pad_maximum_fusion.4), channel_id=1, source_target_pairs={{0,4},{4,8},{8,12},{12,16},{16,20},{20,24},{24,28},{1,5},{5,9},{9,... | collective-permute-start | bytes 6291464 | tf_op jit(solution)/shard_map/ppermute | solution.py:21
  12.5 154.4 %collective-permute-start.1 = (bf16[1,2,512,1024]{3,2,1,0:T(8,128)(2,1)}, bf16[1,2,512,1024]{3,2,1,0:T(8,128)(2,1)}, u32[]{:S(2)}, u32[]{:S(2)}) collective-permute-start(bf16[1,2,512,1024]{3,2,1,0:T(8,128)(2,1)} %pad_maximum_fusion.4), channel_id=1, source_target_pairs={{0,8},{4,12},{8,16},{12,20},{16,24},{20,28},{1,9},{5,13},{9,17},{1... | collective-permute-start | bytes 6291464 | tf_op jit(solution)/shard_map/ppermute | solution.py:21
  16.9 150.0 %collective-permute-start = (bf16[1,2,512,1024]{3,2,1,0:T(8,128)(2,1)}, bf16[1,2,512,1024]{3,2,1,0:T(8,128)(2,1)}, u32[]{:S(2)}, u32[]{:S(2)}) collective-permute-start(bf16[1,2,512,1024]{3,2,1,0:T(8,128)(2,1)} %pad_maximum_fusion.4), channel_id=1, source_target_pairs={{0,12},{4,16},{8,20},{12,24},{16,28},{1,13},{5,17},{9,21},{13,25},... | collective-permute-start | bytes 6291464 | tf_op jit(solution)/shard_map/ppermute | solution.py:21
  22.3 83.9 %all-to-all-start = ((s32[1,8,32]{2,0,1:T(1,128)}), s32[1,8,32]{2,0,1:T(1,128)S(1)}, u32[]{:S(2)}, u32[]{:S(2)}) async-start(s32[1,8,32]{2,0,1:T(1,128)} %sub.69), calls=%async_computation | async-start | bytes 8192 | tf_op jit(solution)/shard_map/all_to_all | solution.py:381
  29.5 76.8 %copy-start.6 = (bf16[1,512,1024]{2,1,0:T(8,128)(2,1)S(1)}, bf16[1,512,1024]{2,1,0:T(8,128)(2,1)}, u32[]{:S(2)}) copy-start(bf16[1,512,1024]{2,1,0:T(8,128)(2,1)} %param.28) | copy-start | bytes 3145732
  117.3 28.9 %copy-start.15 = (pred[1,512,2048]{2,1,0:T(8,128)(4,1)S(1)}, pred[1,512,2048]{2,1,0:T(8,128)(4,1)}, u32[]{:S(2)}) copy-start(pred[1,512,2048]{2,1,0:T(8,128)(4,1)} %and_and_fusion) | copy-start | bytes 3145732
  119.9 41.8 %all-to-all-start.1 = ((bf16[1,2,8,32,1024]{4,3,1,0,2:T(8,128)(2,1)}), bf16[1,2,8,32,1024]{4,3,1,0,2:T(8,128)(2,1)}, u32[]{:S(2)}, u32[]{:S(2)}) async-start(bf16[1,2,8,32,1024]{4,3,1,0,2:T(8,128)(2,1)} %pad_maximum_fusion.7), calls=%async_computation.1 | async-start | bytes 2097152 | tf_op jit(solution)/shard_map/all_to_all | solution.py:50
  147.8 19.1 %copy-start.17 = (bf16[1,1,512,1024]{3,2,1,0:T(8,128)(2,1)S(1)}, bf16[1,1,512,1024]{3,2,1,0:T(8,128)(2,1)}, u32[]{:S(2)}) copy-start(bf16[1,1,512,1024]{3,2,1,0:T(8,128)(2,1)} %copy-done.16) | copy-start | bytes 3145732
  205.1 17.7 %copy-start.5 = (bf16[1,1,2048,1024]{2,3,1,0:T(8,128)(2,1)S(1)}, bf16[1,1,2048,1024]{2,3,1,0:T(8,128)(2,1)}, u32[]{:S(2)}) copy-start(bf16[1,1,2048,1024]{2,3,1,0:T(8,128)(2,1)} %copy.129) | copy-start | bytes 12582916
  205.1 17.7 %copy-start.20 = (bf16[256,8,128]{0,2,1:T(8,128)(2,1)S(1)}, bf16[256,8,128]{0,2,1:T(8,128)(2,1)}, u32[]{:S(2)}) copy-start(bf16[256,8,128]{0,2,1:T(8,128)(2,1)} %copy.107) | copy-start | bytes 1572868
  222.7 15.2 %copy-start.8 = (bf16[1,512,1024]{2,1,0:T(8,128)(2,1)S(1)}, bf16[1,512,1024]{2,1,0:T(8,128)(2,1)}, u32[]{:S(2)}) copy-start(bf16[1,512,1024]{2,1,0:T(8,128)(2,1)} %param.17) | copy-start | bytes 3145732
  222.8 15.2 %copy-start.21 = (bf16[1024,1024]{1,0:T(8,128)(2,1)S(1)}, bf16[1024,1024]{1,0:T(8,128)(2,1)}, u32[]{:S(2)}) copy-start(bf16[1024,1024]{1,0:T(8,128)(2,1)} %param.23) | copy-start | bytes 6291460
  237.9 10.4 %slice-start.5 = ((s8[5767168]{0:T(1024)(128)(4,1)}), s8[4194304]{0:T(1024)(128)(4,1)S(1)}, s32[]{:S(2)}) async-start(s8[5767168]{0:T(1024)(128)(4,1)} %bitcast.284), calls=%async_computation.8 | async-start | bytes 8388608
  239.3 37.8 %copy-start.3 = (f32[512,1024]{1,0:T(8,128)}, f32[512,1024]{1,0:T(8,128)S(1)}, u32[]{:S(2)}) copy-start(f32[512,1024]{1,0:T(8,128)S(1)} %get-tuple-element.102) | copy-start | bytes 6291460
  248.3 16.5 %slice-start.3 = ((s8[5767168]{0:T(1024)(128)(4,1)}), s8[4194304]{0:T(1024)(128)(4,1)S(1)}, s32[]{:S(2)}) async-start(s8[5767168]{0:T(1024)(128)(4,1)} %bitcast.282), calls=%async_computation.6 | async-start | bytes 8388608
  253.3 11.5 %slice-start.4 = ((s8[5767168]{0:T(1024)(128)(4,1)}), s8[1572864]{0:T(1024)(128)(4,1)S(1)}, s32[]{:S(2)}) async-start(s8[5767168]{0:T(1024)(128)(4,1)} %bitcast.282), calls=%async_computation.7 | async-start | bytes 3145728
  328.4 31.0 %copy-start.11 = (bf16[512,1024]{0,1:T(8,128)(2,1)S(1)}, bf16[512,1024]{0,1:T(8,128)(2,1)}, u32[]{:S(2)}) copy-start(bf16[512,1024]{0,1:T(8,128)(2,1)} %copy.132) | copy-start | bytes 3145732
  383.9 41.7 %copy-start.19 = (bf16[8,128,512]{2,1,0:T(8,128)(2,1)}, bf16[8,128,512]{2,1,0:T(8,128)(2,1)S(1)}, u32[]{:S(2)}) copy-start(bf16[8,128,512]{2,1,0:T(8,128)(2,1)S(1)} %multiply_convert_fusion.4) | copy-start | bytes 3145732
  401.2 10.6 %copy-start.1 = (f32[1,1,2048,1024]{2,3,1,0:T(8,128)}, f32[1,1,2048,1024]{2,3,1,0:T(8,128)S(1)}, u32[]{:S(2)}) copy-start(f32[1,1,2048,1024]{2,3,1,0:T(8,128)S(1)} %slice_bitcast_fusion) | copy-start | bytes 25165828
  415.9 9.7 %copy-start.36 = (bf16[1024,1024]{1,0:T(8,128)(2,1)S(1)}, bf16[1024,1024]{1,0:T(8,128)(2,1)}, u32[]{:S(2)}) copy-start(bf16[1024,1024]{1,0:T(8,128)(2,1)} %param.20) | copy-start | bytes 6291460
  421.7 118.8 %collective-permute-start.5 = (bf16[1,2,512,1024]{2,3,1,0:T(8,128)(2,1)}, bf16[1,2,512,1024]{2,3,1,0:T(8,128)(2,1)}, u32[]{:S(2)}, u32[]{:S(2)}) collective-permute-start(bf16[1,2,512,1024]{2,3,1,0:T(8,128)(2,1)} %get-tuple-element.81), channel_id=1, source_target_pairs={{12,0},{16,4},{20,8},{24,12},{28,16},{13,1},{17,5},{21,9},{25,13},... | collective-permute-start | bytes 6291464 | tf_op jit(solution)/shard_map/ppermute | solution.py:21
  423.0 117.6 %collective-permute-start.4 = (bf16[1,2,512,1024]{2,3,1,0:T(8,128)(2,1)}, bf16[1,2,512,1024]{2,3,1,0:T(8,128)(2,1)}, u32[]{:S(2)}, u32[]{:S(2)}) collective-permute-start(bf16[1,2,512,1024]{2,3,1,0:T(8,128)(2,1)} %get-tuple-element.82), channel_id=1, source_target_pairs={{8,0},{12,4},{16,8},{20,12},{24,16},{28,20},{9,1},{13,5},{17,9},{2... | collective-permute-start | bytes 6291464 | tf_op jit(solution)/shard_map/ppermute | solution.py:21
  424.3 116.3 %collective-permute-start.3 = (bf16[1,2,512,1024]{2,3,1,0:T(8,128)(2,1)}, bf16[1,2,512,1024]{2,3,1,0:T(8,128)(2,1)}, u32[]{:S(2)}, u32[]{:S(2)}) collective-permute-start(bf16[1,2,512,1024]{2,3,1,0:T(8,128)(2,1)} %get-tuple-element.80), channel_id=1, source_target_pairs={{4,0},{8,4},{12,8},{16,12},{20,16},{24,20},{28,24},{5,1},{9,5},{13... | collective-permute-start | bytes 6291464 | tf_op jit(solution)/shard_map/ppermute | solution.py:21
  432.3 12.2 %copy-start.9 = (bf16[1,512,1024]{2,1,0:T(8,128)(2,1)S(1)}, bf16[1,512,1024]{2,1,0:T(8,128)(2,1)}, u32[]{:S(2)}) copy-start(bf16[1,512,1024]{2,1,0:T(8,128)(2,1)} %param.17) | copy-start | bytes 3145732
  432.4 12.2 %copy-start.30 = (f32[1024]{0:T(1024)S(1)}, f32[1024]{0:T(1024)}, u32[]{:S(2)}) copy-start(f32[1024]{0:T(1024)} %copy-done.29) | copy-start | bytes 12292
  432.4 12.2 %copy-start.32 = (f32[512]{0:T(512)S(1)}, f32[512]{0:T(512)}, u32[]{:S(2)}) copy-start(f32[512]{0:T(512)} %copy-done.31) | copy-start | bytes 6148
  435.0 93.0 %all-to-all-start.2 = ((bf16[1,2,8,32,1024]{4,3,1,0,2:T(8,128)(2,1)}), bf16[1,2,8,32,1024]{4,3,1,0,2:T(8,128)(2,1)}, u32[]{:S(2)}, u32[]{:S(2)}) async-start(bf16[1,2,8,32,1024]{4,3,1,0,2:T(8,128)(2,1)} %copy.125), calls=%async_computation.2 | async-start | bytes 2097152 | tf_op jit(solution)/shard_map/all_to_all | solution.py:463
  444.6 11.2 %slice-start.7 = ((s8[5767168]{0:T(1024)(128)(4,1)}), s8[4194304]{0:T(1024)(128)(4,1)S(1)}, s32[]{:S(2)}) async-start(s8[5767168]{0:T(1024)(128)(4,1)} %bitcast.286), calls=%async_computation.10 | async-start | bytes 8388608
  702.6 10.7 %copy-start.14 = (f32[512,1024]{1,0:T(8,128)S(1)}, f32[512,1024]{1,0:T(8,128)}, u32[]{:S(2)}) copy-start(f32[512,1024]{1,0:T(8,128)} %copy-done.12) | copy-start | bytes 6291460
  (30 other events, 155.9 us)

commit v2 on v1

v2 whole, which is shorter than its diff:
```python
import functools
import math

import jax
import jax.numpy as jnp
from jax import lax
from jax.experimental import pallas as pl
from jax.experimental.pallas import tpu as pltpu
from jax.sharding import PartitionSpec as P

HEADS = 8
HEAD_DIM = 128
TOPK = 128
BPS = 4
NEG = -1000000000.0
MESH = pl.DeviceIdType.MESH
UNIT = 256
SKEW = 2

def flip(value, bit):
    return value + bit - 2 * bit * ((value // bit) % 2)


def partners():
    seq, doc = lax.axis_index("seq"), lax.axis_index("doc")
    return {
        "core": (flip(seq, 1), doc),
        "x": (flip(seq, 2), doc),
        "y": (flip(seq, 4), doc),
        "low": (seq, flip(doc, 1)),
        "high": (seq, flip(doc, 2)),
    }


ORDERS = (("x", "y", "low", "high"), ("y", "x", "low", "high"), ("low", "high", "x", "y"))


def rs_kernel(plan, every, names, refs_in, gains_in, refs_out, gains_out, own, stages, gain_buf, sems):
    seq, doc = lax.axis_index("seq"), lax.axis_index("doc")
    bits = {
        "core": seq % 2,
        "x": (seq // 2) % 2,
        "y": (seq // 4) % 2,
        "low": doc % 2,
        "high": (doc // 2) % 2,
    }
    peer = partners()
    local_sem, send_sem, recv_sem, gain_send, gain_recv = sems
    barrier = pltpu.get_barrier_semaphore()
    for name in ("core", "x", "y", "low", "high"):
        pl.semaphore_signal(barrier, inc=1, device_id=peer[name], device_id_type=MESH)
    pl.semaphore_wait(barrier, 5)

    def pick(cls, level, unit, side):
        order = ORDERS[cls]
        ref = stages[cls][level]
        name = order[level]
        where = (1 - bits[name]) if side == "send" else bits[name]
        left = [axis for axis in ("y", "x", "high", "low") if axis not in order[:level]]
        index = (unit,) + (slice(None),) * left.index(name) + (where,)
        return ref, index

    def first(cls, unit, array, column):
        source = refs_in[array]
        lanes = pl.ds(column, UNIT)
        there = source.at[:, :, 1 - bits["core"], :, :, :, lanes]
        here = source.at[:, :, bits["core"], :, :, :, lanes]
        local = pltpu.make_async_copy(here, own[cls].at[unit], local_sem[cls].at[unit])
        remote = pltpu.make_async_remote_copy(
            src_ref=there, dst_ref=stages[cls][0].at[unit],
            send_sem=send_sem[cls].at[0, unit], recv_sem=recv_sem[cls].at[0, unit],
            device_id=peer["core"], device_id_type=MESH)
        return local, remote

    def later(cls, level, unit):
        ref, index = pick(cls, level - 1, unit, "send")
        return pltpu.make_async_remote_copy(
            src_ref=ref.at[index], dst_ref=stages[cls][level].at[unit],
            send_sem=send_sem[cls].at[level, unit], recv_sem=recv_sem[cls].at[level, unit],
            device_id=peer[ORDERS[cls][level - 1]], device_id_type=MESH)

    def gain_copy(level):
        name = ("core", "x", "y", "low", "high")[level]
        return pltpu.make_async_remote_copy(
            src_ref=gain_buf.at[0, level], dst_ref=gain_buf.at[1, level],
            send_sem=gain_send.at[level], recv_sem=gain_recv.at[level],
            device_id=peer[name], device_id_type=MESH)

    gain_buf[0, 0] = gains_in[...]
    gain_copy(0).start()
    longest = max(len(units) * every[c] for c, units in enumerate(plan))
    for step in range(longest):
        for cls, units in enumerate(plan):
            if step % every[cls] == 0 and step // every[cls] < len(units):
                array, column = units[step // every[cls]]
                local, remote = first(cls, step // every[cls], array, column)
                remote.start()
                local.start()

    def arrive(cls, level, unit):
        array, column = plan[cls][0]
        ref = stages[cls][level]
        if level == 0:
            local, remote = first(cls, unit, array, column)
            remote.wait_recv()
            local.wait()
            ref[unit] = ref[unit] + own[cls][unit]
        else:
            later(cls, level, unit).wait_recv()
            prev, index = pick(cls, level - 1, unit, "keep")
            if level < 4:
                ref[unit] = ref[unit] + prev[index]
            else:
                refs_out[cls][unit] = ref[unit].astype(jnp.float32) + prev[index].astype(jnp.float32)
        if level < 4:
            later(cls, level + 1, unit).start()

    def body(step, carry):
        for level in range(4, -1, -1):
            for cls, units in enumerate(plan):
                at = step - level * SKEW
                unit = at // every[cls]
                ok = (at >= 0) & (unit < len(units))
                if every[cls] > 1:
                    ok = ok & (at % every[cls] == 0)

                @pl.when(ok)
                def _():
                    arrive(cls, level, unit)
        for level in range(5):
            @pl.when(step == 3 * level + 2)
            def _():
                gain_copy(level).wait_recv()
                total = gain_buf[0, level] + gain_buf[1, level]
                if level < 4:
                    gain_buf[0, level + 1] = total
                    gain_copy(level + 1).start()
                else:
                    gains_out[...] = total
        return carry

    steps = max(longest, 15 - 4 * SKEW) + 4 * SKEW
    lax.fori_loop(0, steps, body, 0)
    for level in range(5):
        gain_copy(level).wait_send()
    for cls, units in enumerate(plan):
        def drain(unit, carry):
            first(cls, unit, *plan[cls][0])[1].wait_send()
            for level in range(1, 5):
                later(cls, level, unit).wait_send()
            return carry
        lax.fori_loop(0, len(units), drain, 0)


def make_rs(plan, every, n_in):
    rows = (32, 32, 88)
    n = [len(p) for p in plan]
    def shapes(cls):
        u, r = n[cls], rows[cls]
        return [(u,) + (2,) * k + (r, UNIT) for k in (4, 3, 2, 1, 0)]

    def kernel(*refs):
        refs_in = refs[:n_in]
        gains_in = refs[n_in]
        refs_out = refs[n_in + 1 : n_in + 4]
        gains_out = refs[n_in + 4]
        k = n_in + 5
        own = refs[k : k + 3]
        k += 3
        stages = [refs[k + 5 * c : k + 5 * c + 5] for c in range(3)]
        k += 15
        gain_buf = refs[k]
        k += 1
        sems = (refs[k : k + 3], refs[k + 3 : k + 6], refs[k + 6 : k + 9], refs[k + 9], refs[k + 10])
        rs_kernel(plan, every, None, refs_in, gains_in, refs_out, gains_out, own, stages, gain_buf, sems)

    scratch = [pltpu.VMEM(shapes(c)[0], jnp.bfloat16) for c in range(3)]
    for c in range(3):
        scratch += [pltpu.VMEM(s, jnp.bfloat16) for s in shapes(c)]
    scratch.append(pltpu.VMEM((2, 5, 16, 128), jnp.float32))
    scratch += [pltpu.SemaphoreType.DMA((n[c],)) for c in range(3)]
    scratch += [pltpu.SemaphoreType.DMA((5, n[c])) for c in range(3)]
    scratch += [pltpu.SemaphoreType.DMA((5, n[c])) for c in range(3)]
    scratch += [pltpu.SemaphoreType.DMA((5,)), pltpu.SemaphoreType.DMA((5,))]
    return pl.pallas_call(
        kernel,
        out_shape=tuple(jax.ShapeDtypeStruct((n[c], rows[c], UNIT), jnp.float32) for c in range(3))
        + (jax.ShapeDtypeStruct((16, 128), jnp.float32),),
        in_specs=[pl.BlockSpec(memory_space=pl.ANY)] * n_in + [pl.BlockSpec(memory_space=pltpu.VMEM)],
        out_specs=tuple(pl.BlockSpec(memory_space=pltpu.VMEM) for _ in range(4)),
        scratch_shapes=scratch,
        name="weight_sums",
        compiler_params=pltpu.CompilerParams(collective_id=0, has_side_effects=True, vmem_limit_bytes=58 * 2**20),
    )


def weight_plan():
    a = [(0, 256 * i) for i in range(11)] + [(2, 256 * i) for i in range(4)] + [(3, 256 * i) for i in range(4)]
    b = [(1, 256 * i) for i in range(11)] + [(4, 256 * i) for i in range(4)] + [(5, 256 * i) for i in range(4)]
    c = [(6, 256 * i) for i in range(4)]
    return (a, b, c), (1, 1, 4)


def reduce_weights(gate, up, query, key, value, out, down, gain_one, gain_two):
    plan, every = weight_plan()
    def wide(g):
        return g.reshape(2, 2, 2, 2, 2, g.shape[0] // 32, g.shape[1])
    gains = jnp.concatenate((gain_one, gain_two)).reshape(16, 128)
    ins = [wide(gate), wide(up), wide(query), wide(key), wide(value), wide(out), wide(down), gains]
    a, b, c, gsum = make_rs(plan, every, 7)(*ins)
    def cols(x):
        return x.transpose(1, 0, 2).reshape(x.shape[1], -1)
    index = lax.axis_index("seq") * lax.axis_size("doc") + lax.axis_index("doc")
    gsum = gsum.reshape(2, 32, 32)
    mine = lax.dynamic_index_in_dim(gsum, index, 1, keepdims=False)
    return (cols(a[:11]), cols(b[:11]), cols(a[11:15]), cols(a[15:19]), cols(b[11:15]), cols(b[15:19]), cols(c), mine[0], mine[1])


HALF = HEADS // 2
LOG2E = math.log2(math.e)
SCALE = HEAD_DIM ** (-0.5)
NT = (((1,), (1,)), ((), ()))
TN = (((0,), (0,)), ((), ()))
NN = (((1,), (0,)), ((), ()))


def matmul(left, right, dims):
    return lax.dot_general(left, right, dims, preferred_element_type=jnp.float32)


def seats():
    seq, doc = lax.axis_index("seq"), lax.axis_index("doc")
    core, chip = seq % 2, (seq // 2) % 2
    mate = (flip(seq, 1), doc)
    across = (flip(seq, 2), doc)
    diagonal = (flip(flip(seq, 2), 1), doc)
    return core, chip, mate, across, diagonal


def meet(peers):
    barrier = pltpu.get_barrier_semaphore()
    for peer in peers:
        pl.semaphore_signal(barrier, inc=1, device_id=peer, device_id_type=MESH)
    pl.semaphore_wait(barrier, len(peers))


def head_lanes(core, head):
    return pl.ds(pl.multiple_of((core * HALF + head) * HEAD_DIM, HEAD_DIM), HEAD_DIM)


def remote(src, dst, send, recv, peer):
    return pltpu.make_async_remote_copy(
        src_ref=src, dst_ref=dst, send_sem=send, recv_sem=recv, device_id=peer, device_id_type=MESH
    )


def share_heads(sources, boxes, core, mate, local_sem, send_sem, recv_sem):
    copies = []
    for i, (source, box) in enumerate(zip(sources, boxes)):
        for head in range(HALF):
            copies.append(
                remote(
                    source.at[:, head_lanes(1 - core, head)],
                    box.at[core, head],
                    send_sem.at[i, head],
                    recv_sem.at[i, head],
                    mate,
                )
            )
            copies[-1].start()
    for i, (source, box) in enumerate(zip(sources, boxes)):
        for head in range(HALF):
            copies.append(
                pltpu.make_async_copy(
                    source.at[:, head_lanes(core, head)], box.at[core, head], local_sem.at[i, head]
                )
            )
            copies[-1].start()
    return copies


def masked(scores, first_key, limit, diagonal):
    key = lax.broadcasted_iota(jnp.int32, scores.shape, 0)
    ok = key + first_key < limit
    if diagonal:
        ok = ok & (key <= lax.broadcasted_iota(jnp.int32, scores.shape, 1))
    return jnp.where(ok, scores, NEG)


def soften(parts):
    top = functools.reduce(
        jnp.maximum, [jnp.max(scores, axis=0, keepdims=True) for scores, _ in parts]
    )
    total, mixed = 0.0, 0.0
    for scores, values in parts:
        exponent = jnp.exp2(scores - top)
        total = total + jnp.sum(exponent, axis=0, keepdims=True)
        mixed = mixed + matmul(values, exponent.astype(jnp.bfloat16), TN)
    return mixed / total, top + jnp.log(total) * LOG2E


def forward_kernel(
    limit_ref, q, k, v, mk, mv,
    attended, qb, kb, vb, qx, mkb, mvb, ob, lse,
    mixed_own, mixed_out, mixed_in, lse_out, lse_in,
    local_sem, mate_send, mate_recv, far_send, far_recv, back_send, back_recv, end_sem,
):
    core, chip, mate, across, diagonal = seats()
    block = q.shape[0]
    limit = limit_ref[0]
    meet((mate, across, diagonal))

    def query_copy(head, own):
        return remote(
            q.at[:, head_lanes(core if own else 1 - core, head)],
            qx.at[core, head],
            far_send.at[0 if own else 1, head],
            far_recv.at[core, head],
            across if own else diagonal,
        )

    def arrived_query(far, head):
        return remote(
            q.at[:, head_lanes(core, head)], qx.at[far, head], far_send.at[0, head], far_recv.at[far, head], across
        )

    @pl.when(chip == 1)
    def _():
        for head in range(HALF):
            query_copy(head, True).start()
            query_copy(head, False).start()

    copies = share_heads((q, k, v, mk, mv), (qb, kb, vb, mkb, mvb), core, mate, local_sem, mate_send, mate_recv)
    for copy in copies:
        copy.wait()

    def own_part(blk, head):
        query = qb[blk, head]
        parts = []
        for kblk in range(blk + 1):
            scores = matmul(kb[kblk, head], query, NT) * (SCALE * LOG2E)
            scores = masked(scores, (2 * chip + kblk) * block, limit, kblk == blk)
            parts.append((scores, vb[kblk, head]))
        parts.append((matmul(mkb[blk, head], query, NT) * (SCALE * LOG2E), mvb[blk, head]))
        return soften(parts)

    for blk in range(2):
        def own_head(head, carry):
            mixed, level = own_part(blk, head)
            mixed_own[blk, head] = mixed
            lse[blk, head] = level
            return carry
        lax.fori_loop(0, HALF, own_head, 0)

    def back_copy(blk, head):
        return (
            remote(mixed_out.at[blk, head], mixed_in.at[blk, head], back_send.at[0, blk, head], back_recv.at[0, blk, head], across),
            remote(lse_out.at[blk, head], lse_in.at[blk, head], back_send.at[1, blk, head], back_recv.at[1, blk, head], across),
        )

    @pl.when(chip == 0)
    def _():
        def cross(i, carry):
            head, blk = i // 2, i % 2
            arrived_query(blk, head).wait_recv()
            query = qx[blk, head]
            parts = []
            for kblk in range(2):
                scores = matmul(kb[kblk, head], query, NT) * (SCALE * LOG2E)
                parts.append((masked(scores, kblk * block, limit, False), vb[kblk, head]))
            mixed, level = soften(parts)
            mixed_out[blk, head] = mixed.astype(jnp.bfloat16)
            lse_out[blk, head] = level
            for copy in back_copy(blk, head):
                copy.start()
            return carry
        lax.fori_loop(0, 2 * HALF, cross, 0)

        def finish(i, carry):
            head, blk = i // 2, i % 2
            ob[blk, head] = mixed_own[blk, head].T.astype(jnp.bfloat16)
            return carry
        lax.fori_loop(0, 2 * HALF, finish, 0)

    @pl.when(chip == 1)
    def _():
        def merge(i, carry):
            head, blk = i // 2, i % 2
            for copy in back_copy(blk, head):
                copy.wait_recv()
            near, far = lse[blk, head], lse_in[blk, head]
            top = jnp.maximum(near, far)
            near, far = jnp.exp2(near - top), jnp.exp2(far - top)
            total = near + far
            mixed = (mixed_own[blk, head] * near + mixed_in[blk, head].astype(jnp.float32) * far) / total
            ob[blk, head] = mixed.T.astype(jnp.bfloat16)
            lse[blk, head] = top + jnp.log(total) * LOG2E
            return carry
        lax.fori_loop(0, 2 * HALF, merge, 0)

    ends = []
    for head in range(HALF):
        ends.append(
            remote(ob.at[1 - core, head], attended.at[:, head_lanes(core, head)], end_sem.at[0, head], end_sem.at[1, head], mate)
        )
        ends.append(
            pltpu.make_async_copy(ob.at[core, head], attended.at[:, head_lanes(core, head)], end_sem.at[2, head])
        )
    for copy in ends:
        copy.start()
    for copy in ends:
        copy.wait()

    @pl.when(chip == 0)
    def _():
        for head in range(HALF):
            for blk in range(2):
                for copy in back_copy(blk, head):
                    copy.wait_send()

    @pl.when(chip == 1)
    def _():
        for head in range(HALF):
            query_copy(head, True).wait_send()
            query_copy(head, False).wait_send()


def attend_forward(limit, queries, keys, values, mem_keys, mem_values):
    block, width = queries.shape
    topk = mem_keys.shape[0]
    low, full = jnp.bfloat16, jnp.float32
    box = (2, HALF, block, HEAD_DIM)
    mem_box = (2, HALF, topk, HEAD_DIM)
    flat = (2, HALF, HEAD_DIM, block)
    row = (2, HALF, 1, block)
    dma = pltpu.SemaphoreType.DMA
    hbm, vmem = pl.BlockSpec(memory_space=pl.ANY), pl.BlockSpec(memory_space=pltpu.VMEM)
    struct = jax.ShapeDtypeStruct
    return pl.pallas_call(
        forward_kernel,
        out_shape=(
            struct((block, width), low),
            struct(box, low), struct(box, low), struct(box, low), struct(box, low),
            struct(mem_box, low), struct(mem_box, low), struct(box, low), struct(row, full),
        ),
        in_specs=[pl.BlockSpec(memory_space=pltpu.SMEM)] + [hbm] * 5,
        out_specs=(hbm,) + (vmem,) * 8,
        scratch_shapes=[
            pltpu.VMEM(flat, full), pltpu.VMEM(flat, low), pltpu.VMEM(flat, low),
            pltpu.VMEM(row, full), pltpu.VMEM(row, full),
            dma((5, HALF)), dma((5, HALF)), dma((5, HALF)),
            dma((2, HALF)), dma((2, HALF)), dma((2, 2, HALF)), dma((2, 2, HALF)), dma((3, HALF)),
        ],
        name="attend_forward",
        compiler_params=pltpu.CompilerParams(collective_id=1, has_side_effects=True, vmem_limit_bytes=56 * 2**20),
    )(limit, queries, keys, values, mem_keys, mem_values)


def backward_kernel(
    limit_ref, grad, qb, kb, vb, qx, mkb, mvb, ob, lse,
    dq, dk, dv, dmk, dmv,
    gb, gx, delta, lse_in, delta_in, dq_own, dq_out, dq_in, dk_sum, dv_sum, dmk_low, dmv_low, dqb, dkb, dvb,
    local_sem, mate_send, mate_recv, far_send, far_recv, row_send, row_recv, back_send, back_recv,
    end_local, end_send, end_recv,
):
    core, chip, mate, across, diagonal = seats()
    block = grad.shape[0]
    limit = limit_ref[0]
    meet((mate, across, diagonal))

    def grad_copy(head, own):
        return remote(
            grad.at[:, head_lanes(core if own else 1 - core, head)],
            gx.at[core, head],
            far_send.at[0 if own else 1, head],
            far_recv.at[core, head],
            across if own else diagonal,
        )

    def arrived_grad(far, head):
        return remote(
            grad.at[:, head_lanes(core, head)], gx.at[far, head], far_send.at[0, head], far_recv.at[far, head], across
        )

    def row_copies():
        return (
            remote(lse, lse_in, row_send.at[0], row_recv.at[0], across),
            remote(delta, delta_in, row_send.at[1], row_recv.at[1], across),
        )

    @pl.when(chip == 1)
    def _():
        for head in range(HALF):
            grad_copy(head, True).start()
            grad_copy(head, False).start()

    copies = share_heads((grad,), (gb,), core, mate, local_sem, mate_send, mate_recv)
    for copy in copies:
        copy.wait()

    def rows(i, carry):
        head, blk = i // 2, i % 2
        product = gb[blk, head].astype(jnp.float32) * ob[blk, head].astype(jnp.float32)
        delta[blk, head] = jnp.sum(product.T, axis=0, keepdims=True)
        return carry

    lax.fori_loop(0, 2 * HALF, rows, 0)

    @pl.when(chip == 1)
    def _():
        for copy in row_copies():
            copy.start()

    def pull(key_rows, value_rows, query, grad_rows, level, inner, where):
        scores = matmul(key_rows, query, NT) * (SCALE * LOG2E)
        if where is not None:
            scores = masked(scores, where[0], limit, where[1])
        weights = jnp.exp2(scores - level)
        grad_weights = matmul(value_rows, grad_rows, NT)
        grad_scores = (weights * (grad_weights - inner)).astype(jnp.bfloat16)
        return (
            matmul(grad_scores, query, NN),
            matmul(weights.astype(jnp.bfloat16), grad_rows, NN),
            matmul(key_rows, grad_scores, TN),
        )

    for blk in range(2):
        def own_head(head, carry):
            query, grad_rows = qb[blk, head], gb[blk, head]
            level, inner = lse[blk, head], delta[blk, head]
            total = 0.0
            for kblk in range(blk + 1):
                gk, gv, gq = pull(
                    kb[kblk, head], vb[kblk, head], query, grad_rows, level, inner,
                    ((2 * chip + kblk) * block, kblk == blk),
                )
                if kblk == blk:
                    dk_sum[kblk, head], dv_sum[kblk, head] = gk, gv
                else:
                    dk_sum[kblk, head] += gk
                    dv_sum[kblk, head] += gv
                total = total + gq
            gk, gv, gq = pull(mkb[blk, head], mvb[blk, head], query, grad_rows, level, inner, None)
            dmk_low[blk, head] = (gk * SCALE).astype(jnp.bfloat16)
            dmv_low[blk, head] = gv.astype(jnp.bfloat16)
            dq_own[blk, head] = total + gq
            return carry
        lax.fori_loop(0, HALF, own_head, 0)

    def back_copy(blk, head):
        return remote(dq_out.at[blk, head], dq_in.at[blk, head], back_send.at[blk, head], back_recv.at[blk, head], across)

    @pl.when(chip == 0)
    def _():
        for copy in row_copies():
            copy.wait_recv()

        def cross(i, carry):
            head, blk = i // 2, i % 2
            arrived_grad(blk, head).wait_recv()
            query, grad_rows = qx[blk, head], gx[blk, head]
            level, inner = lse_in[blk, head], delta_in[blk, head]
            total = 0.0
            for kblk in range(2):
                gk, gv, gq = pull(
                    kb[kblk, head], vb[kblk, head], query, grad_rows, level, inner, (kblk * block, False)
                )
                dk_sum[kblk, head] += gk
                dv_sum[kblk, head] += gv
                total = total + gq
            dq_out[blk, head] = total.astype(jnp.bfloat16)
            back_copy(blk, head).start()
            return carry
        lax.fori_loop(0, 2 * HALF, cross, 0)

    def finish(i, carry):
        head, blk = i // 2, i % 2
        dqb[blk, head] = (dq_own[blk, head].T * SCALE).astype(jnp.bfloat16)
        dkb[blk, head] = (dk_sum[blk, head] * SCALE).astype(jnp.bfloat16)
        dvb[blk, head] = dv_sum[blk, head].astype(jnp.bfloat16)
        return carry

    @pl.when(chip == 1)
    def _():
        def merge(i, carry):
            head, blk = i // 2, i % 2
            back_copy(blk, head).wait_recv()
            dq_own[blk, head] += dq_in[blk, head].astype(jnp.float32)
            return finish(i, carry)
        lax.fori_loop(0, 2 * HALF, merge, 0)

    @pl.when(chip == 0)
    def _():
        lax.fori_loop(0, 2 * HALF, finish, 0)

    ends = []
    for i, (box, out) in enumerate(((dqb, dq), (dkb, dk), (dvb, dv), (dmk_low, dmk), (dmv_low, dmv))):
        for head in range(HALF):
            lanes = head_lanes(core, head)
            ends.append(remote(box.at[1 - core, head], out.at[:, lanes], end_send.at[i, head], end_recv.at[i, head], mate))
            ends.append(pltpu.make_async_copy(box.at[core, head], out.at[:, lanes], end_local.at[i, head]))
    for copy in ends:
        copy.start()
    for copy in ends:
        copy.wait()

    @pl.when(chip == 0)
    def _():
        for head in range(HALF):
            for blk in range(2):
                back_copy(blk, head).wait_send()

    @pl.when(chip == 1)
    def _():
        for copy in row_copies():
            copy.wait_send()
        for head in range(HALF):
            grad_copy(head, True).wait_send()
            grad_copy(head, False).wait_send()


def attend_backward(limit, grad, saved):
    block, width = grad.shape
    topk = saved[4].shape[2]
    low, full = jnp.bfloat16, jnp.float32
    box = (2, HALF, block, HEAD_DIM)
    mem_box = (2, HALF, topk, HEAD_DIM)
    flat = (2, HALF, HEAD_DIM, block)
    row = (2, HALF, 1, block)
    dma = pltpu.SemaphoreType.DMA
    hbm, vmem = pl.BlockSpec(memory_space=pl.ANY), pl.BlockSpec(memory_space=pltpu.VMEM)
    struct = jax.ShapeDtypeStruct
    return pl.pallas_call(
        backward_kernel,
        out_shape=(struct((block, width), low),) * 3 + (struct((topk, width), low),) * 2,
        in_specs=[pl.BlockSpec(memory_space=pltpu.SMEM), hbm] + [vmem] * 8,
        out_specs=(hbm,) * 5,
        scratch_shapes=[
            pltpu.VMEM(box, low), pltpu.VMEM(box, low),
            pltpu.VMEM(row, full), pltpu.VMEM(row, full), pltpu.VMEM(row, full),
            pltpu.VMEM(flat, full), pltpu.VMEM(flat, low), pltpu.VMEM(flat, low),
            pltpu.VMEM(box, full), pltpu.VMEM(box, full),
            pltpu.VMEM(mem_box, low), pltpu.VMEM(mem_box, low),
            pltpu.VMEM(box, low), pltpu.VMEM(box, low), pltpu.VMEM(box, low),
            dma((1, HALF)), dma((1, HALF)), dma((1, HALF)),
            dma((2, HALF)), dma((2, HALF)), dma((2,)), dma((2,)),
            dma((2, HALF)), dma((2, HALF)),
            dma((5, HALF)), dma((5, HALF)), dma((5, HALF)),
        ],
        name="attend_backward",
        compiler_params=pltpu.CompilerParams(collective_id=2, has_side_effects=True, vmem_limit_bytes=56 * 2**20),
    )(limit, grad, *saved)


EPS = 1e-05


def rms_factor(values):
    return lax.rsqrt(jnp.mean(values * values, axis=-1, keepdims=True) + EPS)


def dot32(left, right):
    return jnp.dot(left, right, preferred_element_type=jnp.float32)


def sum_weights(weights, gains):
    if (lax.axis_size("seq"), lax.axis_size("doc")) == (8, 4):
        return reduce_weights(*[grad.astype(jnp.bfloat16) for grad in weights], *gains)
    return tuple(
        lax.psum_scatter(grad, ("seq", "doc"), scatter_dimension=0, tiled=True)
        for grad in weights + gains
    )


def exchange(rows, owner_count, capacity):
    parts, _, width = rows.shape
    shaped = rows.reshape(parts, owner_count, capacity, width)
    moved = lax.all_to_all(shaped, "seq", split_axis=1, concat_axis=1, tiled=True)
    return moved.reshape(parts, owner_count * capacity, width)


def on_device(
    tokens,
    cotangent,
    attn_gain,
    w_query,
    w_key,
    w_value,
    w_out,
    ffn_gain,
    w_gate,
    w_up,
    w_down,
    mem_keys,
    mem_values,
    seg_len,
    mem_idx,
):
    low = jnp.bfloat16
    stream_count, block_len, model_width = tokens.shape
    mem_rows = mem_keys.shape[1]
    seq_count = lax.axis_size("seq")
    segment = lax.axis_index("seq") // BPS
    capacity = 2 * TOPK // seq_count
    slot_count = seq_count * capacity
    limit = lax.dynamic_index_in_dim(seg_len, segment, 1, keepdims=False)

    chosen = mem_idx[0, 0]
    owner = chosen // mem_rows
    order = jnp.arange(TOPK)
    same_before = (owner[:, None] == owner[None, :]) & (order[None, :] < order[:, None])
    slot = owner * capacity + jnp.sum(same_before.astype(jnp.int32), axis=1)
    placed = slot[:, None] == jnp.arange(slot_count)[None, :]
    request = jnp.sum(jnp.where(placed, (chosen % mem_rows)[:, None] + 1, 0), axis=0) - 1
    requested = lax.all_to_all(
        request.reshape(seq_count, capacity), "seq", split_axis=0, concat_axis=0, tiled=True
    ).reshape(slot_count)
    picked = (requested[:, None] == jnp.arange(mem_rows)[None, :]).astype(low)
    placed = placed.astype(low)
    sent = jnp.stack((dot32(picked, mem_keys[0]).astype(low), dot32(picked, mem_values[0]).astype(low)))
    arrived = exchange(sent, seq_count, capacity)
    mem_key_rows = dot32(placed, arrived[0]).astype(low)
    mem_value_rows = dot32(placed, arrived[1]).astype(low)

    tokens_f = tokens[0].astype(jnp.float32)
    gain_one = attn_gain.astype(jnp.float32)
    gain_two = ffn_gain.astype(jnp.float32)
    factor_one = rms_factor(tokens_f)
    unit_one = tokens_f * factor_one
    normed_one = (unit_one * gain_one).astype(low)
    queries = dot32(normed_one, w_query).astype(low)
    keys = dot32(normed_one, w_key).astype(low)
    values = dot32(normed_one, w_value).astype(low)
    attended, *saved = attend_forward(limit, queries, keys, values, mem_key_rows, mem_value_rows)
    middle = tokens_f + dot32(attended, w_out)
    factor_two = rms_factor(middle)
    unit_two = middle * factor_two
    normed_two = (unit_two * gain_two).astype(low)
    gate = dot32(normed_two, w_gate)
    upper = dot32(normed_two, w_up)
    sigma = jax.nn.sigmoid(gate)
    hidden = (gate * sigma * upper).astype(low)
    layer_out = (middle + dot32(hidden, w_down)).astype(low)

    grad_y_low = cotangent[0]
    grad_y = grad_y_low.astype(jnp.float32)
    grad_down = dot32(hidden.T, grad_y_low)
    grad_hidden = dot32(grad_y_low, w_down.T)
    grad_gate_act = (grad_hidden * upper * sigma * (1.0 + gate * (1.0 - sigma))).astype(low)
    grad_up_act = (grad_hidden * gate * sigma).astype(low)
    grad_gate = dot32(normed_two.T, grad_gate_act)
    grad_up = dot32(normed_two.T, grad_up_act)
    grad_normed_two = dot32(grad_gate_act, w_gate.T) + dot32(grad_up_act, w_up.T)
    grad_ffn_gain = jnp.sum(grad_normed_two * unit_two, axis=0)
    scaled_two = gain_two * grad_normed_two
    grad_middle = grad_y + factor_two * (
        scaled_two - unit_two * jnp.mean(scaled_two * unit_two, axis=-1, keepdims=True)
    )
    grad_branch = grad_middle.astype(low)
    grad_out = dot32(attended.T, grad_branch)
    grad_attended = dot32(grad_branch, w_out.T).astype(low)
    grad_q, grad_k, grad_v, grad_mk, grad_mv = attend_backward(limit, grad_attended, saved)

    back = jnp.stack((dot32(placed.T, grad_mk).astype(low), dot32(placed.T, grad_mv).astype(low)))
    returned = exchange(back, seq_count, capacity)
    grad_mem_keys = dot32(picked.T, returned[0])
    grad_mem_values = dot32(picked.T, returned[1])
    grad_query = dot32(normed_one.T, grad_q)
    grad_key = dot32(normed_one.T, grad_k)
    grad_value = dot32(normed_one.T, grad_v)
    grad_normed_one = dot32(grad_q, w_query.T) + dot32(grad_k, w_key.T) + dot32(grad_v, w_value.T)
    grad_attn_gain = jnp.sum(grad_normed_one * unit_one, axis=0)
    scaled_one = gain_one * grad_normed_one
    grad_input = grad_middle + factor_one * (
        scaled_one - unit_one * jnp.mean(scaled_one * unit_one, axis=-1, keepdims=True)
    )
    grad_tokens = grad_input.astype(low)
    gate_rows, up_rows, query_rows, key_rows, value_rows, out_rows, down_rows, attn_row, ffn_row = sum_weights(
        (grad_gate, grad_up, grad_query, grad_key, grad_value, grad_out, grad_down),
        (grad_attn_gain, grad_ffn_gain),
    )
    return (
        layer_out[None],
        grad_tokens[None],
        attn_row,
        query_rows,
        key_rows,
        value_rows,
        out_rows,
        ffn_row,
        gate_rows,
        up_rows,
        down_rows,
        grad_mem_keys[None],
        grad_mem_values[None],
    )


def solution(mesh):
    in_specs = (
        P("doc", "seq", None),
        P("doc", "seq", None),
        P(),
        P(),
        P(),
        P(),
        P(),
        P(),
        P(),
        P(),
        P(),
        P("doc", "seq", None),
        P("doc", "seq", None),
        P("doc", None),
        P("doc", "seq", None),
    )
    out_specs = (
        P("doc", "seq", None),
        P("doc", "seq", None),
        P(("seq", "doc")),
        P(("seq", "doc"), None),
        P(("seq", "doc"), None),
        P(("seq", "doc"), None),
        P(("seq", "doc"), None),
        P(("seq", "doc")),
        P(("seq", "doc"), None),
        P(("seq", "doc"), None),
        P(("seq", "doc"), None),
        P("doc", "seq", None),
        P("doc", "seq", None),
    )
    return jax.shard_map(
        on_device, mesh=mesh, in_specs=in_specs, out_specs=out_specs, check_vma=False
    )
```

time: 726 us -> 383 us (0.53)
  waiting for transfers between devices: 152 us -> 11.4 us
  matrix products: 197 us -> 94.8 us
  Pallas kernels: 139 us -> 223 us
  other arithmetic: 91.1 us -> 12.1 us
  local copies, waits for them, and re-layouts: 80.9 us -> 20.2 us
  starting transfers between devices: 55.6 us -> 13.6 us
    all_to_all x3, waiting for transfers between devices: 152 us -> 11.4 us  [the longest x2 9 us: exchange(): lax.all_to_all(shaped, 'seq', split_axis=1, concat_axis=1, tiled=True)]
    dot_general x27 -> x29, matrix products: 197 us -> 94.8 us  [dot32(): return jnp.dot(left, right, preferred_element_type=jnp.float32)]
    pallas_call x0 -> x2, Pallas kernels: none -> 97.7 us  [the longest x1 57.2 us: attend_backward(): pl.pallas_call(backward_kernel, out_shape=(struct((block, width), low),)...]
    convert_element_type x3 -> x1, other arithmetic: 32.8 us -> 0.24 us  [on_device(): normed_two = (unit_two * gain_two).astype(low)]
    all_to_all x3, starting transfers between devices: 39.2 us -> 13.6 us  [the longest x2 8.47 us: exchange(): lax.all_to_all(shaped, 'seq', split_axis=1, concat_axis=1, tiled=True)]
    reduce_sum x3 -> x2, other arithmetic: 17.9 us -> 0.29 us  [the longest x1 0.17 us: on_device(): slot = owner * capacity + jnp.sum(same_before.astype(jnp.int32), axis=1)]
    ppermute x6 -> x0, starting transfers between devices: 16.3 us -> none  [from_behind(): lax.ppermute(value, axis, [(source, source + steps) for source in range(l...]
    pallas_call x1, Pallas kernels: 139 us -> 125 us  [reduce_weights(): a, b, c, gsum = make_rs(plan, every, 7)(*ins)]
  transfers between devices with their start and end apart: 9 -> 3, of which waited for: 3 -> 3; matrix products, arithmetic and copies ran while one was open for 10% -> 6% of each run, Pallas kernels for 0% -> 0%
where the time goes in v2:
time: 383 us; the launch traced here: 377 us
  Pallas kernels  223 us (58%)
  matrix products  94.8 us (25%)
  local copies, waits for them, and re-layouts  20.2 us (5%)
  starting transfers between devices  13.6 us (4%)
  other arithmetic  12.1 us (3%)
  waiting for transfers between devices  11.4 us (3%)
    pallas_call x1, Pallas kernels, reduce_weights(): a, b, c, gsum = make_rs(plan, every, 7)(*ins)  125 us
    dot_general x29, matrix products, dot32(): return jnp.dot(left, right, preferred_element_type=jnp.float32)  94.8 us
    pallas_call x1, Pallas kernels, attend_backward(): pl.pallas_call(backward_kernel, out_shape=(struct((block, width), low),)...  57.2 us
    pallas_call x1, Pallas kernels, attend_forward(): pl.pallas_call(forward_kernel, out_shape=(struct((block, width), low), st...  40.5 us
    reshape x7, local copies, waits for them, and re-layouts, cols(): return x.transpose(1, 0, 2).reshape(x.shape[1], -1)  9.61 us
    all_to_all x2, waiting for transfers between devices, exchange(): lax.all_to_all(shaped, 'seq', split_axis=1, concat_axis=1, tiled=True)  9 us
    all_to_all x2, starting transfers between devices, exchange(): lax.all_to_all(shaped, 'seq', split_axis=1, concat_axis=1, tiled=True)  8.47 us
  transfers between devices with their start and end apart: 3, of which 3 were waited for; matrix products, arithmetic and copies ran while one was open for 6% of the time, Pallas kernels for 0%

profile of v2, /device:TPU:0, one launch (start us, length us, event | category | flops | bytes accessed | tf_op | source)
XLA Modules:
  0.0 376.6 jit_solution(789794081565525545)
XLA Ops:
  2.5 5.2 %all-to-all-start = ((s32[8,1,32]{2,1,0:T(1,128)}), s32[8,1,32]{2,1,0:T(1,128)S(1)}, u32[]{:S(2)}, u32[]{:S(2)}) async-start(s32[8,1,32]{2,1,0:T(1,128)} %sub.28), calls=%async_computation | async-start | bytes 8192 | tf_op jit(solution)/shard_map/all_to_all | solution.py:715
  9.9 2.4 all-to-all-done
  16.8 4.2 %all-to-all-start.1 = ((bf16[2,8,32,1024]{3,2,0,1:T(8,128)(2,1)}), bf16[2,8,32,1024]{3,2,0,1:T(8,128)(2,1)}, u32[]{:S(2)}, u32[]{:S(2)}) async-start(bf16[2,8,32,1024]{3,2,0,1:T(8,128)(2,1)} %pad_maximum_fusion), calls=%async_computation.1 | async-start | bytes 2097152 | tf_op jit(solution)/shard_map/all_to_all | solution.py:678
  21.1 3.9 %convolution_convert_fusion.10.q = bf16[512,1024]{1,0:T(8,128)(2,1)} fusion(bf16[1024,1024]{1,0:T(8,128)(2,1)} %param.18, bf16[1,512,1024]{2,1,0:T(8,128)(2,1)S(1)} %copy-done.1, f32[1024]{0:T(1024)S(1)} %convert_element_type.97, f32[512]{0:T(512)S(1)} %add_rsqrt_fusion.1), kind=kOutput, calls=%fused_computation.39 | convolution fusion | flops 1076363264 | bytes 4200448 | tf_op jit(solution)/shard_map/dot_general | solution.py:663
  25.5 3.9 %convolution_convert_fusion.9.k = bf16[512,1024]{1,0:T(8,128)(2,1)} fusion(bf16[1024,1024]{1,0:T(8,128)(2,1)} %param.19, bf16[1,512,1024]{2,1,0:T(8,128)(2,1)S(1)} %copy-done.1, f32[1024]{0:T(1024)S(1)} %convert_element_type.97, f32[512]{0:T(512)S(1)} %add_rsqrt_fusion.1), kind=kOutput, calls=%fused_computation.38 | convolution fusion | flops 1076363264 | bytes 4200448 | tf_op jit(solution)/shard_map/dot_general | solution.py:663
  29.4 2.3 convolution_convert_fusion.8.v
  31.7 4.8 %all-to-all-done.1 = bf16[2,8,32,1024]{3,2,0,1:T(8,128)(2,1)} async-done(((bf16[2,8,32,1024]{3,2,0,1:T(8,128)(2,1)}), bf16[2,8,32,1024]{3,2,0,1:T(8,128)(2,1)}, u32[]{:S(2)}, u32[]{:S(2)}) %all-to-all-start.1) | async-done | bytes 1048608 | tf_op jit(solution)/shard_map/all_to_all | solution.py:678
  39.7 40.5 %attend_forward.1 = (bf16[512,1024]{1,0:T(8,128)(2,1)}, bf16[2,4,512,128]{3,2,1,0:T(8,128)(2,1)}, bf16[2,4,512,128]{3,2,1,0:T(8,128)(2,1)}, bf16[2,4,512,128]{3,...) custom-call(s32[1]{0:T(128)} %bitcast.1.limit_ref, ...), custom_call_target="tpu_custom_call" | custom-call | tf_op jit(solution)/shard_map/attend_forward/pallas_call | solution.py:439
  80.3 2.7 multiply_reduce_fusion.2
  83.3 5.0 %fusion.41 = f32[512,2816]{1,0:T(8,128)} fusion(bf16[512,1024]{1,0:T(8,128)(2,1)S(1)} %multiply_convert_fusion.3, bf16[1024,2816]{1,0:T(8,128)(2,1)S(1)} %bitcast.172), kind=kOutput, calls=%fused_computation.98 | convolution fusion | flops 2952790016 | bytes 12582912 | tf_op jit(solution)/shard_map/dot_general | solution.py:663
  88.3 5.0 %fusion.42 = f32[512,2816]{1,0:T(8,128)} fusion(bf16[512,1024]{1,0:T(8,128)(2,1)S(1)} %multiply_convert_fusion.3, bf16[1024,2816]{1,0:T(8,128)(2,1)S(1)} %bitcast.174), kind=kOutput, calls=%fused_computation.99 | convolution fusion | flops 2952790016 | bytes 12582912 | tf_op jit(solution)/shard_map/dot_general | solution.py:663
  93.3 11.8 %multiply_convert_fusion = (bf16[512,2816]{1,0:T(8,128)(2,1)}, bf16[512,2816]{1,0:T(8,128)(2,1)}, bf16[512,2816]{1,0:T(8,128)(2,1)}) fusion(f32[512,2816]{1,0:T(8,128)} %fusion.41, f32[512,2816]{1,0:T(8,128)} %fusion.42, bf16[2816,1024]{1,0:T(8,128)(2,1)} %param.25, bf16[1,512,1024]{2,1,0:T(8,128)(2,1)S(1)} %copy-done.6), kind=kOutput, calls=%fused_computation | convolution fusion | flops 2975858688 | bytes 27000832 | tf_op jit(solution)/shard_map/dot_general | solution.py:663
  105.1 5.1 %fusion.43 = f32[512,1024]{1,0:T(8,128)S(1)} fusion(bf16[512,2816]{1,0:T(8,128)(2,1)} %get-tuple-element.54, bf16[1024,2816]{1,0:T(8,128)(2,1)S(1)} %bitcast.172), kind=kOutput, calls=%fused_computation.100 | convolution fusion | flops 2952790016 | bytes 10747904 | tf_op jit(solution)/shard_map/dot_general | solution.py:663
  110.2 5.1 %convolution_convert_fusion.2 = bf16[1024,2816]{1,0:T(8,128)(2,1)} fusion(bf16[512,1024]{1,0:T(8,128)(2,1)S(1)} %multiply_convert_fusion.3, bf16[512,2816]{1,0:T(8,128)(2,1)S(1)} %copy-done.23), kind=kOutput, calls=%fused_computation.6 | convolution fusion | flops 2955673600 | bytes 9699328 | tf_op jit(solution)/shard_map/dot_general | solution.py:663
  115.3 5.3 %convolution_convert_fusion.1 = bf16[1024,2816]{1,0:T(8,128)(2,1)} fusion(bf16[512,1024]{1,0:T(8,128)(2,1)S(1)} %multiply_convert_fusion.3, bf16[512,2816]{1,0:T(8,128)(2,1)S(1)} %copy-done.20), kind=kOutput, calls=%fused_computation.5 | convolution fusion | flops 2955673600 | bytes 9699328 | tf_op jit(solution)/shard_map/dot_general | solution.py:663
  120.6 3.5 multiply_reduce_fusion
  125.8 2.3 convolution_convert_fusion.7.grad
  128.0 57.2 %attend_backward.1 = (bf16[512,1024]{1,0:T(8,128)(2,1)}, bf16[512,1024]{1,0:T(8,128)(2,1)}, bf16[512,1024]{1,0:T(8,128)(2,1)}, bf16[128,1024]{1,0:T(8,128)(2,1)}, bf16[128,1024]{1,0:T(8,128)(2,1)}) custom-call(s32[1]{0:T(128)} %bitcast.1.limit_ref, bf16[512,1024]{1,0:T(8,128)(2,1)} %convolution_convert_fusion.7.grad, ...), custom_call_target="tpu_custom_call" | custom-call | tf_op jit(solution)/shard_map/attend_backward/pallas_call | solution.py:633
  185.2 3.3 fusion.44
  188.5 2.7 convolution_convert_fusion.6
  192.5 2.8 convolution_convert_fusion.5
  195.3 2.6 convolution_convert_fusion.3
  197.9 2.8 convolution_convert_fusion.4
  200.7 5.1 %convolution_convert_fusion = bf16[2816,1024]{1,0:T(8,128)(2,1)} fusion(bf16[512,2816]{1,0:T(8,128)(2,1)S(1)} %copy-done.21, bf16[1,512,1024]{2,1,0:T(8,128)(2,1)S(1)} %copy-done.6), kind=kOutput, calls=%fused_computation.4 | convolution fusion | flops 2955673600 | bytes 9699328 | tf_op jit(solution)/shard_map/dot_general | solution.py:663
  205.8 3.1 fusion.10
  209.5 125.5 %weight_sums.1 = (f32[19,32,256]{2,1,0:T(8,128)}, f32[19,32,256]{2,1,0:T(8,128)}, f32[4,88,256]{2,1,0:T(8,128)}, f32[16,128]{1,0:T(8,128)}) custom-call(bf16[2,2,2,2,2,32,2816]{6,5,4,3,2,1,0:T(8,128)(2,1)} %bitcast.146, bf16[2,2,2,2,2,32,2816]{6,5,4,3,2,1,0:T(8,128)(2,1)} %bitcast.147, bf16[2,2,2,2,2,32,1024]{6,5,4,3,2,1,0:T(8,128)(2,1)} %bitcast.149, ...), custom_call_target="tpu_custom_call" | custom-call | tf_op jit(solution)/shard_map/weight_sums/pallas_call | solution.py:210
  335.0 1.9 slice_bitcast_fusion.2
  336.9 1.9 slice_bitcast_fusion
  351.7 4.2 %all-to-all-start.2 = ((bf16[2,8,32,1024]{3,2,0,1:T(8,128)(2,1)}), bf16[2,8,32,1024]{3,2,0,1:T(8,128)(2,1)}, u32[]{:S(2)}, u32[]{:S(2)}) async-start(bf16[2,8,32,1024]{3,2,0,1:T(8,128)(2,1)} %pad_maximum_fusion.1), calls=%async_computation.2 | async-start | bytes 2097152 | tf_op jit(solution)/shard_map/all_to_all | solution.py:678
  355.9 3.9 %fusion.13 = bf16[1,512,1024]{2,1,0:T(8,128)(2,1)} fusion(f32[512,1024]{1,0:T(8,128)} %copy-done.4, f32[512,1024]{1,0:T(8,128)} %get-tuple-element.71, bf16[1,512,1024]{2,1,0:T(8,128)(2,1)S(1)} %copy-done.1, f32[512]{0:T(512)S(1)} %copy-done.11, f32[1024]{0:T(1024)S(1)} %convert_element_type.97, f32[512]{0:T(512)S(1)} %add_rsqrt_fusion.1), kind=kLoop, calls=%fused_computation.47 | loop fusion | flops 4194304 | bytes 6299648 | tf_op jit(solution)/shard_map/broadcast_in_dim | solution.py:784
  360.4 6.7 %fusion.12 = bf16[1,512,1024]{2,1,0:T(8,128)(2,1)} fusion(f32[512,1024]{1,0:T(8,128)S(1)} %copy-done.3, bf16[512,2816]{1,0:T(8,128)(2,1)S(1)} %copy-done.22, bf16[2816,1024]{1,0:T(8,128)(2,1)} %param.25), kind=kOutput, calls=%fused_computation.40 | convolution fusion | flops 2953838592 | bytes 11796480 | tf_op jit(solution)/shard_map/dot_general | solution.py:663
  367.1 4.2 %all-to-all-done.2 = bf16[2,8,32,1024]{3,2,0,1:T(8,128)(2,1)} async-done(((bf16[2,8,32,1024]{3,2,0,1:T(8,128)(2,1)}), bf16[2,8,32,1024]{3,2,0,1:T(8,128)(2,1)}, u32[]{:S(2)}, u32[]{:S(2)}) %all-to-all-start.2) | async-done | bytes 1048608 | tf_op jit(solution)/shard_map/all_to_all | solution.py:678
  (100 shorter events, 34.6 us)
Async XLA Ops:
  0.6 28.7 %copy-start = (bf16[1024,1024]{1,0:T(8,128)(2,1)S(1)}, bf16[1024,1024]{1,0:T(8,128)(2,1)}, u32[]{:S(2)}) copy-start(bf16[1024,1024]{1,0:T(8,128)(2,1)} %param.20) | copy-start | bytes 6291460
  0.7 14.6 %copy-start.5 = (bf16[1,512,1024]{2,1,0:T(8,128)(2,1)S(1)}, bf16[1,512,1024]{2,1,0:T(8,128)(2,1)}, u32[]{:S(2)}) copy-start(bf16[1,512,1024]{2,1,0:T(8,128)(2,1)} %param.26) | copy-start | bytes 3145732
  2.5 9.8 %all-to-all-start = ((s32[8,1,32]{2,1,0:T(1,128)}), s32[8,1,32]{2,1,0:T(1,128)S(1)}, u32[]{:S(2)}, u32[]{:S(2)}) async-start(s32[8,1,32]{2,1,0:T(1,128)} %sub.28), calls=%async_computation | async-start | bytes 8192 | tf_op jit(solution)/shard_map/all_to_all | solution.py:715
  15.7 5.3 %copy-start.1 = (bf16[1,512,1024]{2,1,0:T(8,128)(2,1)S(1)}, bf16[1,512,1024]{2,1,0:T(8,128)(2,1)}, u32[]{:S(2)}) copy-start(bf16[1,512,1024]{2,1,0:T(8,128)(2,1)} %param.15) | copy-start | bytes 3145732
  16.8 19.7 %all-to-all-start.1 = ((bf16[2,8,32,1024]{3,2,0,1:T(8,128)(2,1)}), bf16[2,8,32,1024]{3,2,0,1:T(8,128)(2,1)}, u32[]{:S(2)}, u32[]{:S(2)}) async-start(bf16[2,8,32,1024]{3,2,0,1:T(8,128)(2,1)} %pad_maximum_fusion), calls=%async_computation.1 | async-start | bytes 2097152 | tf_op jit(solution)/shard_map/all_to_all | solution.py:678
  21.0 3.9 %copy-start.12 = (bf16[1024]{0:T(1024)(128)(2,1)S(1)}, bf16[1024]{0:T(1024)(128)(2,1)}, u32[]{:S(2)}) copy-start(bf16[1024]{0:T(1024)(128)(2,1)} %param.22) | copy-start | bytes 6148
  21.1 3.9 %copy-start.19 = (s32[1,2]{1,0:T(1,128)S(1)}, s32[1,2]{1,0:T(1,128)}, u32[]{:S(2)}) copy-start(s32[1,2]{1,0:T(1,128)} %param.28) | copy-start | bytes 28
  38.7 41.5 %copy-start.13 = (bf16[1024,1024]{1,0:T(8,128)(2,1)S(1)}, bf16[1024,1024]{1,0:T(8,128)(2,1)}, u32[]{:S(2)}) copy-start(bf16[1024,1024]{1,0:T(8,128)(2,1)} %param.21) | copy-start | bytes 6291460
  80.3 3.0 slice-start
  80.3 3.0 slice-start.1
  83.0 41.1 %copy-start.2 = (f32[512,1024]{1,0:T(8,128)}, f32[512,1024]{1,0:T(8,128)S(1)}, u32[]{:S(2)}) copy-start(f32[512,1024]{1,0:T(8,128)S(1)} %get-tuple-element.69) | copy-start | bytes 6291460
  83.0 5.3 %slice-start.2 = ((s8[5767168]{0:T(1024)(128)(4,1)}), s8[4194304]{0:T(1024)(128)(4,1)S(1)}, s32[]{:S(2)}) async-start(s8[5767168]{0:T(1024)(128)(4,1)} %bitcast.173), calls=%async_computation.5 | async-start | bytes 8388608
  83.3 5.0 %slice-start.3 = ((s8[5767168]{0:T(1024)(128)(4,1)}), s8[1572864]{0:T(1024)(128)(4,1)S(1)}, s32[]{:S(2)}) async-start(s8[5767168]{0:T(1024)(128)(4,1)} %bitcast.173), calls=%async_computation.6 | async-start | bytes 3145728
  88.3 5.0 %copy-start.6 = (bf16[1,512,1024]{2,1,0:T(8,128)(2,1)S(1)}, bf16[1,512,1024]{2,1,0:T(8,128)(2,1)}, u32[]{:S(2)}) copy-start(bf16[1,512,1024]{2,1,0:T(8,128)(2,1)} %param.16) | copy-start | bytes 3145732
  105.1 5.1 %copy-start.23 = (bf16[512,2816]{1,0:T(8,128)(2,1)S(1)}, bf16[512,2816]{1,0:T(8,128)(2,1)}, u32[]{:S(2)}) copy-start(bf16[512,2816]{1,0:T(8,128)(2,1)} %get-tuple-element.54) | copy-start | bytes 8650756
  110.2 5.1 %copy-start.20 = (bf16[512,2816]{1,0:T(8,128)(2,1)S(1)}, bf16[512,2816]{1,0:T(8,128)(2,1)}, u32[]{:S(2)}) copy-start(bf16[512,2816]{1,0:T(8,128)(2,1)} %get-tuple-element.53) | copy-start | bytes 8650756
  124.2 1.6 copy-start.14
  125.8 69.6 %copy-start.4 = (f32[512,1024]{1,0:T(8,128)}, f32[512,1024]{1,0:T(8,128)S(1)}, u32[]{:S(2)}) copy-start(f32[512,1024]{1,0:T(8,128)S(1)} %multiply_add_fusion) | copy-start | bytes 6291460
  185.2 3.3 copy-start.18
  188.5 2.7 copy-start.15
  188.5 2.7 copy-start.17
  192.5 2.8 copy-start.16
  195.3 2.6 copy-start.7
  197.9 2.8 copy-start.21
  340.1 8.9 %copy-start.8 = (f32[4,88,256]{2,1,0:T(8,128)S(1)}, f32[4,88,256]{2,1,0:T(8,128)}, u32[]{:S(2)}) copy-start(f32[4,88,256]{2,1,0:T(8,128)} %get-tuple-element.46) | copy-start | bytes 1081348
  340.1 9.6 %copy-start.10 = (bf16[128,1024]{1,0:T(8,128)(2,1)S(1)}, bf16[128,1024]{1,0:T(8,128)(2,1)}, u32[]{:S(2)}) copy-start(bf16[128,1024]{1,0:T(8,128)(2,1)} %get-tuple-element.48) | copy-start | bytes 786436
  340.1 10.0 %copy-start.9 = (bf16[128,1024]{1,0:T(8,128)(2,1)S(1)}, bf16[128,1024]{1,0:T(8,128)(2,1)}, u32[]{:S(2)}) copy-start(bf16[128,1024]{1,0:T(8,128)(2,1)} %get-tuple-element.47) | copy-start | bytes 786436
  350.6 5.3 %copy-start.11 = (f32[512]{0:T(512)S(1)}, f32[512]{0:T(512)}, u32[]{:S(2)}) copy-start(f32[512]{0:T(512)} %broadcast_multiply_fusion) | copy-start | bytes 6148
  351.7 19.7 %all-to-all-start.2 = ((bf16[2,8,32,1024]{3,2,0,1:T(8,128)(2,1)}), bf16[2,8,32,1024]{3,2,0,1:T(8,128)(2,1)}, u32[]{:S(2)}, u32[]{:S(2)}) async-start(bf16[2,8,32,1024]{3,2,0,1:T(8,128)(2,1)} %pad_maximum_fusion.1), calls=%async_computation.2 | async-start | bytes 2097152 | tf_op jit(solution)/shard_map/all_to_all | solution.py:678
  355.9 4.5 %copy-start.3 = (f32[512,1024]{1,0:T(8,128)S(1)}, f32[512,1024]{1,0:T(8,128)}, u32[]{:S(2)}) copy-start(f32[512,1024]{1,0:T(8,128)} %copy-done.2) | copy-start | bytes 6291460
  355.9 4.4 %copy-start.22 = (bf16[512,2816]{1,0:T(8,128)(2,1)S(1)}, bf16[512,2816]{1,0:T(8,128)(2,1)}, u32[]{:S(2)}) copy-start(bf16[512,2816]{1,0:T(8,128)(2,1)} %get-tuple-element.55) | copy-start | bytes 8650756
